TPU v7x, 256 devices: a whole 4x4x8 slice. The times are simulated.
256 devices in a mesh: tx: 32 (over y, z_hi, core), ty: 8 (over x, z_lo).
Axes of the slice: x: 4, y: 4, z: 8 (z_hi: 4, z_lo: 2; z = z_hi * 2 + z_lo), core: 2. Of those that a mesh axis runs over, the one named last changes fastest.
Arguments:
- cells: bfloat16 [32, 8, 512, 512], P('tx', 'ty'), may hold values from -6 to 6
- halo_inputs: bfloat16 [32, 8, 256, 512], P('tx', 'ty'), may hold values from -6 to 6
- stale_halo: bfloat16 [32, 8, 1, 256, 512], P('tx', 'ty'), may hold values from -6 to 6
- stale_returned: bfloat16 [32, 8, 1, 256, 512], P('tx', 'ty'), may hold values from -3 to 3
- cotangent: bfloat16 [32, 8, 512, 512], P('tx', 'ty'), may hold values from -6 to 6
- expression: bfloat16 [32, 8, 512, 512], P('tx', 'ty'), may hold values from -6 to 6
- halo_expression: bfloat16 [32, 8, 256, 512], P('tx', 'ty'), may hold values from -6 to 6
- neighbours: int32 [32, 8, 16, 512], P('tx', 'ty'), may hold values from 0 to 767
- edge_mask: int32 [32, 8, 16, 512], P('tx', 'ty'), may hold values 0 or 1
- send_rows: int32 [32, 8, 8, 32], P('tx', 'ty'), may hold values from 0 to 511
- live_cells: int32 [32, 8], P('tx', 'ty'), may hold values from 256 to 512
- ligand_genes: int32 [1024], replicated, may hold values from 0 to 511
- receptor_genes: int32 [1024], replicated, may hold values from 0 to 511
- gate_weights: float32 [1024], replicated, may hold values from -0.1875 to 0.1875
- self_weights: bfloat16 [2, 512, 512], replicated, may hold values from -0.25 to 0.25
- neighbour_weights: bfloat16 [2, 512, 512], replicated, may hold values from -0.25 to 0.25
Outputs:
- fresh_halo: bfloat16 [32, 8, 1, 256, 512], P('tx', 'ty')
- returned_grads: bfloat16 [32, 8, 1, 256, 512], P('tx', 'ty')
- layer_updates: float32 [4, 512, 512], replicated
- gate_update: float32 [1024], replicated
All inputs are finite; a program needn't handle non-finite values. No bound on the sum of `edge_mask` on one device may be relied on, other than what follows from the above.
Results may differ from a plain program's by a relative error of at most 0.0062.
Values may be sent and summed in bfloat16 or wider, within the bound.
No kernel may reach another device: no remote copies, remote signals or barrier semaphores. Data moves between devices by JAX's collectives and lax.ppermute only.
A program may use at most 64 MiB of HBM per device.

v0:
```python
import jax
import jax.numpy as jnp
from jax import lax
from jax.sharding import PartitionSpec as P

OFFSETS = ((-1, -1), (-1, 0), (-1, 1), (0, -1), (0, 1), (1, -1), (1, 0), (1, 1))
HIGHEST = lax.Precision.HIGHEST


def from_behind(value, axis, steps):
    count = lax.axis_size(axis)
    leading, last = (max(0, -steps), min(count, count - steps))
    return lax.ppermute(value, axis, [(source, source + steps) for source in range(leading, last)])


def silu_slope(pre_act):
    sigmoid_value = jax.nn.sigmoid(pre_act)
    return sigmoid_value * (1.0 + pre_act * (1.0 - sigmoid_value))


def along_wide(payload, offset):
    return from_behind(payload, "tx", offset)


def along_narrow(payload, offset):
    return from_behind(payload, "ty", offset)


def route_blocks(blocks, block_axis):
    pieces = {}
    for direction, offset in enumerate(OFFSETS):
        pieces[offset] = lax.index_in_dim(blocks, direction, block_axis, keepdims=False)

    def offset_of(lead_offset, cross_offset):
        return (lead_offset, cross_offset)

    passed = {}
    for lead_offset in (-1, 1):
        payload = jnp.stack(
            [pieces[offset_of(lead_offset, cross_offset)] for cross_offset in (-1, 0, 1)]
        )
        shifted = along_wide(payload, lead_offset)
        for position, cross_offset in enumerate((-1, 0, 1)):
            passed[offset_of(lead_offset, cross_offset)] = shifted[position]
    arrived = {offset_of(-1, 0): passed[offset_of(-1, 0)], offset_of(1, 0): passed[offset_of(1, 0)]}
    for cross_offset in (-1, 1):
        payload = jnp.stack(
            [
                pieces[offset_of(0, cross_offset)],
                passed[offset_of(-1, cross_offset)],
                passed[offset_of(1, cross_offset)],
            ]
        )
        shifted = along_narrow(payload, cross_offset)
        arrived[offset_of(0, cross_offset)] = shifted[0]
        arrived[offset_of(-1, cross_offset)] = shifted[1]
        arrived[offset_of(1, cross_offset)] = shifted[2]
    return jnp.stack([arrived[offset] for offset in OFFSETS], block_axis)


def on_device(
    cells,
    halo_inputs,
    stale_halo,
    stale_returned,
    cotangent,
    expression,
    halo_expression,
    neighbours,
    edge_mask,
    send_rows,
    live_cells,
    ligand_genes,
    receptor_genes,
    gate_weights,
    self_weights,
    neighbour_weights,
):
    own_state = cells[0, 0]
    halo_first = halo_inputs[0, 0]
    stale_rows = stale_halo[0, 0]
    stale_back = stale_returned[0, 0]
    upstream = cotangent[0, 0]
    genes_here = expression[0, 0]
    genes_halo = halo_expression[0, 0]
    neighbour_ids = neighbours[0, 0]
    valid_edges = edge_mask[0, 0]
    outgoing = send_rows[0, 0]
    live_count = live_cells[0, 0]
    layer_total = self_weights.shape[0]
    cell_count, model_width = own_state.shape
    gene_count = genes_here.shape[1]
    joined_count = cell_count + genes_halo.shape[0]
    joined_ids = jnp.arange(joined_count, dtype=jnp.int32)
    edge_table = (neighbour_ids[:, :, None] == joined_ids[None, None, :]).astype(jnp.float32)

    def dense_edges(values):
        return jnp.sum(values[:, :, None] * edge_table, axis=0)

    def pick_edges(matrix):
        return jnp.sum(edge_table * matrix[None], axis=2)

    gene_ids = jnp.arange(gene_count, dtype=jnp.int32)
    ligand_table = (gene_ids[:, None] == ligand_genes[None, :]).astype(jnp.bfloat16)
    receptor_table = (gene_ids[:, None] == receptor_genes[None, :]).astype(jnp.bfloat16)
    all_genes = jnp.concatenate([genes_here, genes_halo], 0)
    ligand = jnp.dot(all_genes, ligand_table, preferred_element_type=jnp.float32).astype(
        jnp.bfloat16
    )
    receptor = jnp.dot(genes_here, receptor_table, preferred_element_type=jnp.float32).astype(
        jnp.bfloat16
    )
    ligand_wide = ligand.astype(jnp.float32)
    scaled = receptor.astype(jnp.float32) * gate_weights[None, :]
    score_table = jnp.dot(scaled, ligand_wide.T, precision=HIGHEST)
    edge_score = pick_edges(score_table)
    gate_value = jax.nn.sigmoid(edge_score)
    weight = 0.25 * valid_edges.astype(jnp.float32) * gate_value
    adjacency = dense_edges(weight)
    cell_ids = jnp.arange(cell_count, dtype=jnp.int32)
    send_table = (outgoing.reshape(-1)[:, None] == cell_ids[None, :]).astype(jnp.bfloat16)
    states = [own_state]
    full_rows = []
    aggregates = []
    pre_acts = []
    for layer_id in range(layer_total):
        halo_rows = halo_first if layer_id == 0 else stale_rows[layer_id - 1]
        joined = jnp.concatenate([states[layer_id], halo_rows], 0)
        aggregate = jnp.dot(adjacency, joined.astype(jnp.float32), precision=HIGHEST).astype(
            jnp.bfloat16
        )
        pre_act = jnp.dot(
            states[layer_id], self_weights[layer_id], preferred_element_type=jnp.float32
        )
        pre_act = pre_act + jnp.dot(
            aggregate, neighbour_weights[layer_id], preferred_element_type=jnp.float32
        )
        full_rows.append(joined)
        aggregates.append(aggregate)
        pre_acts.append(pre_act)
        if layer_id + 1 < layer_total:
            states.append(
                (states[layer_id].astype(jnp.float32) + jax.nn.silu(pre_act)).astype(jnp.bfloat16)
            )
    send_blocks = jnp.stack(
        [
            jnp.dot(send_table, states[1], preferred_element_type=jnp.float32)
            .astype(jnp.bfloat16)
            .reshape(8, -1, model_width)
        ]
    )
    live_rows = (cell_ids < live_count)[:, None]
    grad_state = jnp.where(live_rows, upstream.astype(jnp.float32), jnp.float32(0.0))
    edge_grad = jnp.zeros(neighbour_ids.shape, jnp.float32)
    layer_grads = [None] * (2 * layer_total)
    halo_grads = []
    for layer_id in range(layer_total - 1, -1, -1):
        grad_pre = (grad_state * silu_slope(pre_acts[layer_id])).astype(jnp.bfloat16)
        layer_grads[2 * layer_id] = jnp.dot(
            states[layer_id].T, grad_pre, preferred_element_type=jnp.float32
        )
        layer_grads[2 * layer_id + 1] = jnp.dot(
            aggregates[layer_id].T, grad_pre, preferred_element_type=jnp.float32
        )
        grad_aggregate = jnp.dot(
            grad_pre, neighbour_weights[layer_id].T, preferred_element_type=jnp.float32
        ).astype(jnp.bfloat16)
        joined = full_rows[layer_id]
        inner_table = jnp.dot(grad_aggregate, joined.T, preferred_element_type=jnp.float32)
        edge_grad = edge_grad + pick_edges(inner_table)
        if layer_id > 0:
            grad_full = jnp.dot(adjacency.T, grad_aggregate.astype(jnp.float32), precision=HIGHEST)
            halo_grads.insert(
                0, grad_full[cell_count:].astype(jnp.bfloat16).reshape(8, -1, model_width)
            )
            grad_state = grad_state + jnp.dot(
                grad_pre, self_weights[layer_id].T, preferred_element_type=jnp.float32
            )
            grad_state = grad_state + grad_full[:cell_count]
            grad_state = grad_state + lax.dot_general(
                send_table,
                stale_back[layer_id - 1],
                (((0,), (0,)), ((), ())),
                preferred_element_type=jnp.float32,
            )
    grad_score = (
        0.25 * valid_edges.astype(jnp.float32) * edge_grad * gate_value * (1.0 - gate_value)
    )
    score_grads = dense_edges(grad_score)
    gate_rows = jnp.dot(score_grads, ligand_wide, precision=HIGHEST)
    gate_grad = jnp.sum(gate_rows * receptor.astype(jnp.float32), axis=0)
    backward_blocks = jnp.flip(jnp.stack(halo_grads), 1)
    combined = route_blocks(jnp.stack([send_blocks, backward_blocks]), 2)
    fresh_blocks = combined[0]
    returned_blocks = jnp.flip(combined[1], 1)
    gradient = jnp.concatenate([jnp.stack(layer_grads).reshape(-1), gate_grad])
    summed_all = lax.psum(gradient, ("tx", "ty"))
    square = jnp.sum(summed_all * summed_all)
    clip_factor = jnp.minimum(1.0, 2.0 * model_width / jnp.sqrt(square + 1e-06))
    update = clip_factor * summed_all
    layer_size = 2 * layer_total * model_width * model_width
    layer_part = update[:layer_size].reshape(2 * layer_total, model_width, model_width)
    gate_part = update[layer_size:]
    halo_shape = (1, 1, layer_total - 1, -1, model_width)
    return (
        fresh_blocks.reshape(halo_shape),
        returned_blocks.reshape(halo_shape),
        layer_part,
        gate_part,
    )


def solution(mesh):
    return jax.shard_map(
        on_device,
        mesh=mesh,
        in_specs=(
            P("tx", "ty", None, None),
            P("tx", "ty", None, None),
            P("tx", "ty", None, None, None),
            P("tx", "ty", None, None, None),
            P("tx", "ty", None, None),
            P("tx", "ty", None, None),
            P("tx", "ty", None, None),
            P("tx", "ty", None, None),
            P("tx", "ty", None, None),
            P("tx", "ty", None, None),
            P("tx", "ty"),
            P(),
            P(),
            P(),
            P(),
            P(),
        ),
        out_specs=(P("tx", "ty", None, None, None), P("tx", "ty", None, None, None), P(), P()),
        check_vma=False,
    )
```

profile of v0, /device:TPU:6, one launch (start us, length us, event | category | flops | bytes accessed | tf_op | source)
XLA Modules:
  0.0 383.7 jit_solution(4572880929984368920)
XLA Ops:
  7.2 0.0 copy-start
  7.2 0.0 all-reduce.2.cloned.1.call-start
  7.3 1.9 fusion.5
  9.2 0.0 copy-start.29
  9.2 1.0 fusion.4
  10.3 1.2 copy-done.30
  11.5 2.9 fusion
  14.4 0.0 copy-start.1
  14.4 4.5 %select_reduce_fusion.4 = f32[16,512]{1,0:T(8,128)S(1)} fusion(f32[512,768]{1,0:T(8,128)S(1)} %fusion, s32[16,512]{1,0:T(8,128)S(1)} %bitcast.169), kind=kLoop, calls=%fused_computation.4 | loop fusion | flops 18866176 | bytes 1638400 | tf_op jit(solution)/shard_map/reduce_sum | solution.py:101
  19.0 3.2 select_reduce_fusion.3
  22.2 0.0 copy-start.23
  22.2 0.4 fusion.27
  22.7 1.4 convolution_convert_fusion.3
  24.1 1.6 add_convert_fusion
  25.7 0.4 fusion.22
  26.2 0.5 copy-done.15
  26.7 1.4 convolution_convert_fusion.2
  28.8 0.8 fusion.12
  29.5 0.8 copy-done.8
  30.3 0.5 convolution_convert_fusion.1
  30.8 1.5 fusion.77
  32.3 0.0 copy-start.4
  32.3 0.8 reverse_bitcast_fusion
  33.2 0.1 eq.56
  33.2 0.3 convolution_convert_fusion.4
  33.6 1.5 fusion.55
  35.2 0.7 pad_maximum_fusion.9
  35.9 2.4 collective-permute-start.1
  38.3 0.7 pad_maximum_fusion.8
  39.0 1.5 collective-permute-start
  40.5 0.6 fusion.31
  41.1 1.5 convolution_bitcast_fusion
  42.6 1.5 convolution_bitcast_fusion.1
  44.1 0.4 fusion.30
  44.5 0.1 copy-done.14
  44.6 0.1 copy-done.26
  44.8 0.8 fusion.9
  45.6 3.3 fusion.10
  48.9 0.5 convolution_bitcast_fusion.2
  49.4 0.5 convolution_bitcast_fusion.3
  49.9 0.5 copy-done.12
  50.3 9.0 %select_reduce_fusion.1 = (f32[16,512]{1,0:T(8,128)S(1)}, f32[16,512]{1,0:T(8,128)S(1)}) fusion(f32[512,768]{1,0:T(8,128)S(1)} %copy-done.12, s32[16,512]{1,0:T(8,128)S(1)} %bitcast.171, f32[512,768]{1,0:T(8,128)S(1)} %fusion.31), kind=kLoop, calls=%fused_computation.1 | loop fusion | flops 31440896 | bytes 3244032 | tf_op jit(solution)/shard_map/reduce_sum | solution.py:101
  59.3 3.2 select_reduce_fusion
  62.5 2.5 pad_maximum_fusion.1
  65.0 5.2 %copy.51 = f32[4,512,512]{2,1,0:T(8,128)} copy(f32[4,512,512]{1,2,0:T(8,128)} %pad_maximum_fusion.1) | data formatting | bytes 8388608 | tf_op jit(solution)/shard_map/stack | solution.py:196
  70.2 3.4 copy.62
  73.7 2.7 fusion.1
  76.4 0.9 fusion.76
  77.3 0.9 fusion.75
  78.2 4.1 %collective-permute-start.2 = (bf16[3,2,1,32,512]{4,3,1,2,0:T(8,128)(2,1)S(1)}, bf16[3,2,1,32,512]{4,3,1,2,0:T(8,128)(2,1)S(1)}, u32[]{:S(2)}, u32[]{:S(2)}) collective-permute-start(bf16[3,2,1,32,512]{4,3,1,2,0:T(8,128)(2,1)S(1)} %pad_maximum_fusion.10), channel_id=1, source_target_pairs={{1,0},{2,1},{3,2},{4,3},{5,4},{6,5},{7,6},{9,8},{10,9},{11,10},{12... | collective-permute-start | bytes 589832 | tf_op jit(solution)/shard_map/ppermute | solution.py:13
  82.3 2.6 pad_maximum_fusion
  84.9 0.0 all-reduce.2.cloned.1.call-update
  85.0 1.9 collective-permute-start.3
  86.9 0.8 fusion.56
  87.8 5.7 %collective-permute-done.3 = bf16[3,2,1,32,512]{4,3,1,2,0:T(8,128)(2,1)S(1)} collective-permute-done((bf16[3,2,1,32,512]{4,3,1,2,0:T(8,128)(2,1)S(1)}, bf16[3,2,1,32,512]{4,3,1,2,0:T(8,128)(2,1)S(1)}, u32[]{:S(2)}, u32[]{:S(2)}) %collective-permute-start.3) | collective-permute-done | bytes 196640 | tf_op jit(solution)/shard_map/ppermute | solution.py:13
  93.5 0.8 fusion.50
  94.3 0.7 slice_bitcast_fusion
  95.1 0.7 rev.8
  95.8 266.9 %all-reduce.2.cloned.1.call-done = f32[1049600]{0:T(1024)} async-done(((f32[1049600]{0:T(1024)}), f32[1049600]{0:T(1024)}) %all-reduce.2.cloned.1.call-update) | async-done | bytes 4198416 | tf_op jit(solution)/shard_map/psum | solution.py:197
  362.6 3.4 multiply_reduce_fusion
  366.7 2.4 broadcast_multiply_fusion
  369.1 2.2 slice.154
  371.3 0.6 slice.155
  371.9 4.9 %reshape.63 = f32[4,512,512]{2,1,0:T(8,128)} reshape(f32[1048576]{0:T(1024)} %slice.154) | data formatting | bytes 8388608 | tf_op jit(solution)/shard_map/reshape | solution.py:202
  (74 shorter events, 0.3 us)
Async XLA Ops:
  7.2 36.9 %copy-start = (bf16[1,1,1,256,512]{4,3,2,1,0:T(8,128)(2,1)S(1)}, bf16[1,1,1,256,512]{4,3,2,1,0:T(8,128)(2,1)}, u32[]{:S(2)}) copy-start(bf16[1,1,1,256,512]{4,3,2,1,0:T(8,128)(2,1)} %param.19) | copy-start | bytes 786436
  7.2 2.0 copy-start.24
  7.2 2.0 copy-start.28
  7.2 2.0 copy-start.27
  7.2 355.4 %all-reduce.2.cloned.1.call-start = ((), (), s32[]{:S(2)}) async-start(), calls=%async_computation | async-start | bytes 8396800 | tf_op jit(solution)/shard_map/psum | solution.py:197
  9.2 1.1 copy-start.32
  9.2 2.2 copy-start.29
  10.3 1.2 copy-start.30
  11.5 2.9 copy-start.17
  11.5 7.5 %copy-start.20 = (s32[1,1,16,512]{3,2,1,0:T(8,128)S(1)}, s32[1,1,16,512]{3,2,1,0:T(8,128)}, u32[]{:S(2)}) copy-start(s32[1,1,16,512]{3,2,1,0:T(8,128)} %param.24) | copy-start | bytes 98308
  14.4 7.8 %copy-start.1 = (bf16[1,1,512,512]{3,2,1,0:T(8,128)(2,1)S(1)}, bf16[1,1,512,512]{3,2,1,0:T(8,128)(2,1)}, u32[]{:S(2)}) copy-start(bf16[1,1,512,512]{3,2,1,0:T(8,128)(2,1)} %param.16) | copy-start | bytes 1572868
  14.4 7.8 %copy-start.13 = (bf16[2,512,512]{2,1,0:T(8,128)(2,1)S(1)}, bf16[2,512,512]{2,1,0:T(8,128)(2,1)}, u32[]{:S(2)}) copy-start(bf16[2,512,512]{2,1,0:T(8,128)(2,1)} %param.30) | copy-start | bytes 3145732
  19.0 3.7 copy-start.19
  22.2 1.9 copy-start.23
  24.1 1.6 copy-start.6
  25.7 1.0 copy-start.15
  25.7 3.0 copy-start.25
  28.1 1.4 copy-start.10
  29.5 0.8 copy-start.8
  30.8 2.4 copy-start.22
  32.3 6.7 %copy-start.4 = (f32[768,512]{1,0:T(8,128)}, f32[768,512]{1,0:T(8,128)S(1)}, u32[]{:S(2)}) copy-start(f32[768,512]{1,0:T(8,128)S(1)} %fusion.77) | copy-start | bytes 4718596
  33.2 7.2 %copy-start.16 = (bf16[1,1,1,256,512]{4,3,2,1,0:T(8,128)(2,1)S(1)}, bf16[1,1,1,256,512]{4,3,2,1,0:T(8,128)(2,1)}, u32[]{:S(2)}) copy-start(bf16[1,1,1,256,512]{4,3,2,1,0:T(8,128)(2,1)} %param.18) | copy-start | bytes 786436
  35.1 5.9 %copy-start.9 = (bf16[512,512]{1,0:T(8,128)(2,1)S(1)}, bf16[512,512]{1,0:T(8,128)(2,1)}, u32[]{:S(2)}) copy-start(bf16[512,512]{1,0:T(8,128)(2,1)} %copy-done.8) | copy-start | bytes 1572868
  35.1 5.9 %copy-start.11 = (bf16[512,512]{1,0:T(8,128)(2,1)S(1)}, bf16[512,512]{1,0:T(8,128)(2,1)}, u32[]{:S(2)}) copy-start(bf16[512,512]{1,0:T(8,128)(2,1)} %copy-done.10) | copy-start | bytes 1572868
  35.9 40.5 %collective-permute-start.1 = (bf16[3,2,1,32,512]{4,3,1,2,0:T(8,128)(2,1)}, bf16[3,2,1,32,512]{4,3,1,2,0:T(8,128)(2,1)}, u32[]{:S(2)}, u32[]{:S(2)}) collective-permute-start(bf16[3,2,1,32,512]{4,3,1,2,0:T(8,128)(2,1)} %pad_maximum_fusion.9), channel_id=1, source_target_pairs={{0,8},{8,16},{16,24},{24,32},{32,40},{40,48},{48,56},{56,64},{64,7... | collective-permute-start | bytes 589832 | tf_op jit(solution)/shard_map/ppermute | solution.py:13
  39.0 38.3 %collective-permute-start = (bf16[3,2,1,32,512]{4,3,1,2,0:T(8,128)(2,1)}, bf16[3,2,1,32,512]{4,3,1,2,0:T(8,128)(2,1)}, u32[]{:S(2)}, u32[]{:S(2)}) collective-permute-start(bf16[3,2,1,32,512]{4,3,1,2,0:T(8,128)(2,1)} %pad_maximum_fusion.8), channel_id=1, source_target_pairs={{8,0},{16,8},{24,16},{32,24},{40,32},{48,40},{56,48},{64,56},{72,6... | collective-permute-start | bytes 589832 | tf_op jit(solution)/shard_map/ppermute | solution.py:13
  41.1 3.4 copy-start.34
  42.6 1.9 copy-start.5
  42.6 2.1 copy-start.14
  42.6 2.2 copy-start.26
  45.6 3.3 copy-start.7
  48.9 1.4 copy-start.12
  50.3 9.0 %copy-start.21 = (s32[1,1,16,512]{3,2,1,0:T(8,128)S(1)}, s32[1,1,16,512]{3,2,1,0:T(8,128)}, u32[]{:S(2)}) copy-start(s32[1,1,16,512]{3,2,1,0:T(8,128)} %param.24) | copy-start | bytes 98308
  50.3 12.2 %copy-start.2 = (f32[1,512,512]{1,2,0:T(8,128)S(1)}, f32[1,512,512]{1,2,0:T(8,128)}, u32[]{:S(2)}) copy-start(f32[1,512,512]{1,2,0:T(8,128)} %convolution_bitcast_fusion) | copy-start | bytes 3145732
  50.3 12.2 %copy-start.3 = (f32[1,512,512]{1,2,0:T(8,128)S(1)}, f32[1,512,512]{1,2,0:T(8,128)}, u32[]{:S(2)}) copy-start(f32[1,512,512]{1,2,0:T(8,128)} %convolution_bitcast_fusion.1) | copy-start | bytes 3145732
  70.2 3.4 copy-start.31
  70.2 3.4 copy-start.33
  73.7 4.5 %copy-start.18 = (bf16[1,2,1,32,512]{4,3,1,2,0:T(8,128)(2,1)S(1)}, bf16[1,2,1,32,512]{4,3,1,2,0:T(8,128)(2,1)}, u32[]{:S(2)}) copy-start(bf16[1,2,1,32,512]{4,3,1,2,0:T(8,128)(2,1)} %get-tuple-element.9) | copy-start | bytes 196612
  78.2 8.7 %collective-permute-start.2 = (bf16[3,2,1,32,512]{4,3,1,2,0:T(8,128)(2,1)S(1)}, bf16[3,2,1,32,512]{4,3,1,2,0:T(8,128)(2,1)S(1)}, u32[]{:S(2)}, u32[]{:S(2)}) collective-permute-start(bf16[3,2,1,32,512]{4,3,1,2,0:T(8,128)(2,1)S(1)} %pad_maximum_fusion.10), channel_id=1, source_target_pairs={{1,0},{2,1},{3,2},{4,3},{5,4},{6,5},{7,6},{9,8},{10,9},{11,10},{12... | collective-permute-start | bytes 589832 | tf_op jit(solution)/shard_map/ppermute | solution.py:13
  85.0 8.5 %collective-permute-start.3 = (bf16[3,2,1,32,512]{4,3,1,2,0:T(8,128)(2,1)S(1)}, bf16[3,2,1,32,512]{4,3,1,2,0:T(8,128)(2,1)S(1)}, u32[]{:S(2)}, u32[]{:S(2)}) collective-permute-start(bf16[3,2,1,32,512]{4,3,1,2,0:T(8,128)(2,1)S(1)} %pad_maximum_fusion.11), channel_id=1, source_target_pairs={{0,1},{1,2},{2,3},{3,4},{4,5},{5,6},{6,7},{8,9},{9,10},{10,11},{11... | collective-permute-start | bytes 589832 | tf_op jit(solution)/shard_map/ppermute | solution.py:13
Sparse Core Ops, SparseCore 0:
  85.0 277.5 all-reduce.1
where the time goes:
time: 384 us
  waiting for transfers between devices  273 us (71%)
  other arithmetic  33.7 us (9%)
  matrix products  25.9 us (7%)
  local copies, waits for them, and re-layouts  25.6 us (7%)
  between operations  16 us (4%)
  starting transfers between devices  9.93 us (3%)
    psum x1, waiting for transfers between devices, on_device(): summed_all = lax.psum(gradient, ('tx', 'ty'))  267 us
    reduce_sum x2, other arithmetic, pick_edges(): return jnp.sum(edge_table * matrix[None], axis=2)  13.5 us
    ppermute x4, starting transfers between devices, from_behind(): lax.ppermute(value, axis, [(source, source + steps) for source in range(l...  9.89 us
    unnamed x78, local copies, waits for them, and re-layouts  8.46 us
  transfers between devices with their start and end apart: 5, of which 2 were waited for; matrix products, arithmetic and copies ran while one was open for 11% of the time, Pallas kernels for 0%

commit v1 on v0

v1 whole, which is shorter than its diff:
```python
import functools

import jax
import jax.numpy as jnp
from jax import lax
from jax.experimental import pallas as pl
from jax.experimental.pallas import tpu as pltpu
from jax.sharding import PartitionSpec as P

F32 = jnp.float32
BF16 = jnp.bfloat16
AXES = ("tx", "ty")


def ring_label(position):
    return position ^ (position >> 1)


def place(index):
    tx, ty = divmod(index, 8)
    y, z_hi, core = tx // 8, (tx // 2) % 4, tx % 2
    x, z_lo = ty // 2, ty % 2
    return x, y, z_hi * 2 + z_lo, core


def index_of(x, y, z, core):
    return (y * 8 + (z // 2) * 2 + core) * 8 + x * 2 + z % 2


def unlabel(label):
    return label ^ (label >> 1)


def xor_pairs(kind, flip):
    pairs = []
    for index in range(256):
        x, y, z, core = place(index)
        if kind == "core":
            core ^= 1
        elif kind == "z":
            label = (z ^ (z >> 1)) ^ flip
            z = label ^ (label >> 1) ^ (label >> 2)
        else:
            along_x = (kind == "first") == (core == 0)
            if along_x:
                x = unlabel(ring_label(x) ^ flip)
            else:
                y = unlabel(ring_label(y) ^ flip)
        pairs.append((index, index_of(x, y, z, core)))
    return pairs


def swap(value, kind, flip=1):
    return lax.ppermute(value, AXES, xor_pairs(kind, flip))


def nn(a, b):
    return lax.dot_general(a, b, (((1,), (0,)), ((), ())), preferred_element_type=F32)


def nt(a, b):
    return lax.dot_general(a, b, (((1,), (1,)), ((), ())), preferred_element_type=F32)


def tn(a, b):
    return lax.dot_general(a, b, (((0,), (0,)), ((), ())), preferred_element_type=F32)


def tile_kernel(
    place_ref, nbr, msk, snd, lig, rec, gwt,
    cells, halo, stale, sback, cot, expr, hexpr, ws, wn,
    o_lm, o_lp, o_mm, o_mp, o_keep, o_send, o_gate,
    full0, full1, xall, sb, ct, wsv, wnv, cnt, adj, slope_g, inner, slope0, agg0, grads, sems,
):
    n, w = ct.shape
    full_n = full0.shape[0]

    def fetch(src, dst, slot):
        copy = pltpu.make_async_copy(src, dst, sems.at[slot])
        copy.start()
        return copy

    c_expr = fetch(expr, xall.at[pl.ds(0, n)], 0)
    c_hexpr = fetch(hexpr, xall.at[pl.ds(n, full_n - n)], 1)
    c_cells = fetch(cells, full0.at[pl.ds(0, n)], 2)
    c_halo = fetch(halo, full0.at[pl.ds(n, full_n - n)], 3)
    c_ws = fetch(ws, wsv, 4)
    c_wn = fetch(wn, wnv, 5)
    c_stale = fetch(stale, full1.at[pl.ds(n, full_n - n)], 6)
    c_cot = fetch(cot, ct, 7)
    c_sb = fetch(sback, sb, 8)

    ids = nbr[...]
    low = jnp.bitwise_and(ids, 127)
    field = jnp.left_shift(msk[...], 5 * jnp.right_shift(ids, 7))
    rows128 = lax.broadcasted_iota(jnp.int32, (128, 128), 0)
    for part in range(n // 128):
        cols = slice(part * 128, part * 128 + 128)
        words = jnp.zeros((128, 128), jnp.int32)
        for k in range(ids.shape[0]):
            words = words + jnp.where(rows128 == low[k : k + 1, cols], field[k : k + 1, cols], 0)
        words = words.T
        for block in range(full_n // 128):
            count = jnp.bitwise_and(jnp.right_shift(words, 5 * block), 31)
            cnt[cols, block * 128 : block * 128 + 128] = (0.25 * count.astype(F32)).astype(BF16)

    genes = xall.shape[1]
    pairs = lig.shape[1]
    gene_rows = lax.broadcasted_iota(jnp.int32, (genes, pairs), 0)
    rec_table = jnp.where(gene_rows == rec[...], gwt[...], 0.0).astype(BF16)
    lig_table = jnp.where(gene_rows == lig[...], 1.0, 0.0).astype(BF16)
    mixed = nt(rec_table, lig_table).astype(BF16)
    c_expr.wait()
    c_hexpr.wait()
    left = nn(xall[0:n], mixed).astype(BF16)
    half_tanh = 0.5 * jnp.tanh(0.5 * nt(left, xall[...]))
    count = cnt[...].astype(F32)
    weight = count * (0.5 + half_tanh)
    adj[...] = weight.astype(BF16)
    slope_g[...] = weight * (0.5 - half_tanh)

    c_cells.wait()
    c_halo.wait()
    state0 = full0[0:n]
    agg0[...] = nn(adj[...], full0[...]).astype(BF16)
    c_ws.wait()
    c_wn.wait()
    pre0 = nn(state0, wsv[0]) + nn(agg0[...], wnv[0])
    sig0 = 0.5 + 0.5 * jnp.tanh(0.5 * pre0)
    slope0[...] = sig0 * (1.0 + pre0 * (1.0 - sig0))
    full1[0:n] = (state0.astype(F32) + pre0 * sig0).astype(BF16)

    c_stale.wait()
    agg1 = nn(adj[...], full1[...]).astype(BF16)
    pre1 = nn(full1[0:n], wsv[1]) + nn(agg1, wnv[1])
    sig1 = 0.5 + 0.5 * jnp.tanh(0.5 * pre1)
    slope1 = sig1 * (1.0 + pre1 * (1.0 - sig1))
    c_cot.wait()
    live = lax.broadcasted_iota(jnp.int32, (n, w), 0) < place_ref[0]
    carried = jnp.where(live, ct[...].astype(F32), 0.0)
    gpre1 = (carried * slope1).astype(BF16)
    grads[2 * n : 3 * n] = tn(full1[0:n], gpre1)
    grads[3 * n : 4 * n] = tn(agg1, gpre1)
    gagg1 = nt(gpre1, wnv[1]).astype(BF16)
    inner[...] = nt(gagg1, full1[...])
    gfull = tn(adj[...], gagg1)
    back = gfull[n:].astype(BF16)

    sent = snd.shape[1]
    send_table = jnp.where(
        lax.broadcasted_iota(jnp.int32, (n, sent), 0) == snd[...], 1.0, 0.0
    ).astype(BF16)
    fresh = tn(send_table, full1[0:n]).astype(BF16)
    b = sent // 8
    o_lm[0] = fresh[0 : 3 * b]
    o_lp[0] = fresh[5 * b : 8 * b]
    o_mm[0] = fresh[3 * b : 4 * b]
    o_mp[0] = fresh[4 * b : 5 * b]
    for pos in range(3):
        o_lm[1, pos * b : (pos + 1) * b] = back[(7 - pos) * b : (8 - pos) * b]
        o_lp[1, pos * b : (pos + 1) * b] = back[(2 - pos) * b : (3 - pos) * b]
    o_mm[1] = back[4 * b : 5 * b]
    o_mp[1] = back[3 * b : 4 * b]

    c_sb.wait()
    carried = carried + nt(gpre1, wsv[1]) + gfull[:n] + nn(send_table, sb[...])
    gpre0 = (carried * slope0[...]).astype(BF16)
    grads[0:n] = tn(state0, gpre0)
    grads[n : 2 * n] = tn(agg0[...], gpre0)
    gagg0 = nt(gpre0, wnv[0]).astype(BF16)
    spread = (slope_g[...] * (inner[...] + nt(gagg0, full0[...]))).astype(BF16)
    gathered = nn(spread, xall[...]).astype(BF16)
    gene_grad = tn(xall[0:n], gathered)
    gene_hi = gene_grad.astype(BF16)
    gene_lo = (gene_grad - gene_hi.astype(F32)).astype(BF16)
    by_pair = nn(gene_hi, lig_table) + nn(gene_lo, lig_table)
    gate = jnp.sum(jnp.where(gene_rows == rec[...], by_pair, 0.0), axis=0, keepdims=True)
    gate8 = jnp.concatenate(
        [gate[:, :w], gate[:, w:], jnp.zeros((6, w), F32)], axis=0
    )
    gate_hi = gate8.astype(BF16)
    gate_lo = (gate8 - gate_hi.astype(F32)).astype(BF16)
    o_gate[...] = gate_hi.astype(F32) + gate_lo.astype(F32)

    core = place_ref[1]
    half = 2 * n
    step = half // 16
    for j in range(16):
        here = pl.multiple_of(core * half + (place_ref[2] ^ j) * step, step)
        there = pl.multiple_of((1 - core) * half + (place_ref[3] ^ j) * step, step)
        o_keep[j * step : (j + 1) * step] = grads[pl.ds(here, step)]
        o_send[j * step : (j + 1) * step] = grads[pl.ds(there, step)].astype(BF16)
    o_send[half:] = jnp.concatenate([gate_hi.astype(F32), gate_lo.astype(F32)], 0).astype(BF16)


def sum_kernel(counts, *refs):
    arrivals, split = counts
    own, gate = refs[0], refs[1]
    got = refs[2 : 2 + arrivals]
    outs = refs[2 + arrivals :]
    rows = own.shape[0]

    def gate_of(ref):
        both = ref[rows : rows + 16].astype(F32)
        return both[0:8] + both[8:16]

    def total(lo, hi):
        value = own[lo:hi]
        for ref in got:
            value = value + ref[lo:hi].astype(F32)
        return value

    if arrivals == 3:
        gates = (gate[...] + gate_of(got[2])) + (gate_of(got[0]) + gate_of(got[1]))
    else:
        gates = gate[...] + gate_of(got[0])
    gate_hi = gates.astype(BF16).astype(F32)
    gate_lo = (gates - gate_hi).astype(BF16).astype(F32)
    if split:
        part = rows // 4
        keep, gate_out, sends = outs[0], outs[1], outs[2:]
        keep[...] = total(0, part)
        gate_out[...] = gate_hi + gate_lo
        for j, ref in enumerate(sends, 1):
            ref[0:part] = total(j * part, (j + 1) * part).astype(BF16)
            ref[part:] = jnp.concatenate([gate_hi, gate_lo], 0).astype(BF16)
    else:
        outs[0][0:rows] = total(0, rows)
        outs[0][rows:] = gates


def add_kernel(a, b, o):
    o[...] = a[...] + b[...]


def last_kernel(place_ref, own, other, gate_own, gate_other, o_layers, o_gate, whole):
    rows, w = own.shape
    core = place_ref[1]
    step = rows // 16
    total = jnp.zeros((8, w), F32)
    for j in range(16):
        here = pl.multiple_of(core * rows + (place_ref[2] ^ j) * step, step)
        there = pl.multiple_of((1 - core) * rows + (place_ref[3] ^ j) * step, step)
        whole[pl.ds(here, step)] = own[j * step : (j + 1) * step].astype(F32)
        whole[pl.ds(there, step)] = other[j * step : (j + 1) * step].astype(F32)
    gate = jnp.where(core == 0, gate_own[...], gate_other[...])
    total = total + gate * gate
    for j in range(32):
        part = whole[j * step : (j + 1) * step]
        square = part * part
        for k in range(step // 8):
            total = total + square[k * 8 : (k + 1) * 8]
    square = jnp.sum(jnp.sum(total, axis=0, keepdims=True), axis=1, keepdims=True)
    clip = jnp.minimum(1.0, (2.0 * w) / jnp.sqrt(square + 1e-06))
    o_layers[...] = whole[...] * clip
    o_gate[...] = gate * clip


def call(kernel, outs, *args, scratch=(), smem=0):
    specs = [pl.BlockSpec(memory_space=pltpu.SMEM)] * smem
    specs += [pl.BlockSpec(memory_space=pltpu.VMEM)] * (len(args) - smem)
    return pl.pallas_call(
        kernel,
        out_shape=outs,
        in_specs=specs,
        out_specs=jax.tree.map(lambda _: pl.BlockSpec(memory_space=pltpu.VMEM), outs),
        scratch_shapes=list(scratch),
        compiler_params=pltpu.CompilerParams(vmem_limit_bytes=48 * 1024 * 1024),
    )(*args)


def shape(rows, w, kind):
    return jax.ShapeDtypeStruct((rows, w), kind)


def from_behind(value, axis, steps):
    count = lax.axis_size(axis)
    first, last = (max(0, -steps), min(count, count - steps))
    return lax.ppermute(value, axis, [(source, source + steps) for source in range(first, last)])


def on_device(
    cells, halo_inputs, stale_halo, stale_returned, cotangent, expression, halo_expression,
    neighbours, edge_mask, send_rows, live_cells, ligand_genes, receptor_genes, gate_weights,
    self_weights, neighbour_weights,
):
    n, w = cells.shape[2:]
    h = halo_inputs.shape[2]
    degree = neighbours.shape[2]
    pairs = ligand_genes.shape[0]
    genes = expression.shape[3]
    b = h // 8

    tx, ty = lax.axis_index("tx"), lax.axis_index("ty")
    x_label, y_label, core = ring_label(ty // 2), ring_label(tx // 8), tx % 2
    x_first, y_first = x_label * 4 + y_label, y_label * 4 + x_label
    mine = jnp.where(core == 0, x_first, y_first)
    partner = jnp.where(core == 0, y_first, x_first)
    where = jnp.stack([live_cells[0, 0], core, mine, partner]).astype(jnp.int32)

    vmem = pl.BlockSpec(memory_space=pltpu.VMEM)
    hbm = pl.BlockSpec(memory_space=pl.ANY)
    outs = (
        jax.ShapeDtypeStruct((2, 3 * b, w), BF16),
        jax.ShapeDtypeStruct((2, 3 * b, w), BF16),
        jax.ShapeDtypeStruct((2, b, w), BF16),
        jax.ShapeDtypeStruct((2, b, w), BF16),
        shape(2 * n, w, F32),
        shape(2 * n + 16, w, BF16),
        shape(8, w, F32),
    )
    lead_m, lead_p, mid_m, mid_p, keep, send, gate = pl.pallas_call(
        tile_kernel,
        out_shape=outs,
        in_specs=[pl.BlockSpec(memory_space=pltpu.SMEM)] + [vmem] * 6 + [hbm] * 9,
        out_specs=(vmem,) * len(outs),
        scratch_shapes=[
            pltpu.VMEM((n + h, w), BF16),
            pltpu.VMEM((n + h, w), BF16),
            pltpu.VMEM((n + h, genes), BF16),
            pltpu.VMEM((h, w), BF16),
            pltpu.VMEM((n, w), BF16),
            pltpu.VMEM((2, w, w), BF16),
            pltpu.VMEM((2, w, w), BF16),
            pltpu.VMEM((n, n + h), BF16),
            pltpu.VMEM((n, n + h), BF16),
            pltpu.VMEM((n, n + h), F32),
            pltpu.VMEM((n, n + h), F32),
            pltpu.VMEM((n, w), F32),
            pltpu.VMEM((n, w), BF16),
            pltpu.VMEM((4 * n, w), F32),
            pltpu.SemaphoreType.DMA((9,)),
        ],
        compiler_params=pltpu.CompilerParams(vmem_limit_bytes=56 * 1024 * 1024),
    )(
        where,
        neighbours.reshape(degree, n),
        edge_mask.reshape(degree, n),
        send_rows.reshape(1, h),
        ligand_genes.reshape(1, pairs),
        receptor_genes.reshape(1, pairs),
        gate_weights.reshape(1, pairs),
        cells.reshape(n, w),
        halo_inputs.reshape(h, w),
        stale_halo.reshape(h, w),
        stale_returned.reshape(h, w),
        cotangent.reshape(n, w),
        expression.reshape(n, genes),
        halo_expression.reshape(h, genes),
        self_weights,
        neighbour_weights,
    )

    got = swap(send, "core")
    part = n // 2
    quarter = [shape(part, w, F32), shape(8, w, F32)] + [shape(part + 16, w, BF16)] * 3
    keep, gate, *sends = call(functools.partial(sum_kernel, (1, True)), quarter, keep, gate, got)
    got = [swap(value, "first", j) for j, value in enumerate(sends, 1)]
    part = part // 4
    quarter = [shape(part, w, F32), shape(8, w, F32)] + [shape(part + 16, w, BF16)] * 3
    keep, gate, *sends = call(functools.partial(sum_kernel, (3, True)), quarter, keep, gate, *got)
    got = [swap(value, "second", j) for j, value in enumerate(sends, 1)]
    both = call(
        functools.partial(sum_kernel, (3, False)), shape(part + 8, w, F32), keep, gate, *got
    )
    for flip in (1, 2, 4):
        both = both + swap(both, "z", flip)
    own, gate = both[:part].astype(BF16), both[part:]
    own = jnp.concatenate([own] + [swap(own, "second", j) for j in (1, 2, 3)], 0)
    own = jnp.concatenate([own] + [swap(own, "first", j) for j in (1, 2, 3)], 0)
    other = swap(own, "core")
    gate_other = swap(gate, "core")

    lead_m = from_behind(lead_m, "tx", -1).reshape(2, 3, b, w)
    lead_p = from_behind(lead_p, "tx", 1).reshape(2, 3, b, w)
    cross_m = jnp.stack([mid_m, lead_m[:, 0], lead_p[:, 0]], 1)
    cross_p = jnp.stack([mid_p, lead_m[:, 2], lead_p[:, 2]], 1)
    cross_m = from_behind(cross_m, "ty", -1)
    cross_p = from_behind(cross_p, "ty", 1)
    arrived = [
        cross_m[:, 1], lead_m[:, 1], cross_p[:, 1], cross_m[:, 0],
        cross_p[:, 0], cross_m[:, 2], lead_p[:, 1], cross_p[:, 2],
    ]
    fresh = jnp.concatenate([value[0] for value in arrived], 0)
    returned = jnp.concatenate([value[1] for value in arrived[::-1]], 0)

    layers, gate = call(
        last_kernel, (shape(4 * n, w, F32), shape(8, w, F32)), where, own, other, gate, gate_other,
        scratch=[pltpu.VMEM((4 * n, w), F32)], smem=1,
    )
    halo_shape = (1, 1, 1, h, w)
    return (
        fresh.reshape(halo_shape),
        returned.reshape(halo_shape),
        layers.reshape(4, n, w),
        gate[:2].reshape(pairs),
    )


def solution(mesh):
    tile = P("tx", "ty")
    return jax.shard_map(
        on_device,
        mesh=mesh,
        in_specs=(tile,) * 11 + (P(),) * 5,
        out_specs=(tile, tile, P(), P()),
        check_vma=False,
    )
```

time: 384 us -> 119 us (0.31)
  waiting for transfers between devices: 273 us -> 45.6 us
  starting transfers between devices: 9.93 us -> 45.3 us
  other arithmetic: 33.7 us -> 2.41 us
  matrix products: 25.9 us -> 0 us
  local copies, waits for them, and re-layouts: 25.6 us -> 4.41 us
  Pallas kernels: 0 us -> 17.3 us
  between operations: 16 us -> 1.57 us
    psum x1 -> x0, waiting for transfers between devices: 267 us -> none  [on_device(): summed_all = lax.psum(gradient, ('tx', 'ty'))]
    ppermute x4 -> x22, waiting for transfers between devices: 5.67 us -> 45.6 us  [the longest x18 43.6 us: swap(): return lax.ppermute(value, AXES, xor_pairs(kind, flip))]
    ppermute x4 -> x22, starting transfers between devices: 9.89 us -> 45.3 us  [the longest x18 35.4 us: swap(): return lax.ppermute(value, AXES, xor_pairs(kind, flip))]
    dot_general x21 -> x0, matrix products: 25.9 us -> none  [the longest x2 3.93 us: on_device(): jnp.dot(grad_aggregate, joined.T, preferred_element_type=jnp.float32)]
    reduce_sum x5 -> x0, other arithmetic: 23.2 us -> none  [the longest x2 13.5 us: pick_edges(): return jnp.sum(edge_table * matrix[None], axis=2)]
    pallas_call x0 -> x5, Pallas kernels: none -> 17.3 us  [the longest x1 13.5 us: on_device(): pl.pallas_call(tile_kernel, out_shape=outs, in_specs=[pl.BlockSpec(memory...]
    another operation x3 -> x0, local copies, waits for them, and re-layouts: 6.06 us -> none  [the longest x1 5.23 us: on_device(): gradient = jnp.concatenate([jnp.stack(layer_grads).reshape(-1), gate_grad])]
    unnamed x78 -> x29, local copies, waits for them, and re-layouts: 8.46 us -> 3.03 us
  transfers between devices with their start and end apart: 5 -> 22, of which waited for: 2 -> 15; matrix products, arithmetic and copies ran while one was open for 11% -> 2% of each run, Pallas kernels for 0% -> 0%
where the time goes in v1:
time: 119 us; the launch traced here: 117 us
  waiting for transfers between devices  45.6 us (38%)
  starting transfers between devices  45.3 us (38%)
  Pallas kernels  17.3 us (15%)
  local copies, waits for them, and re-layouts  4.41 us (4%)
  other arithmetic  2.41 us (2%)
  between operations  1.57 us (1%)
    ppermute x18, waiting for transfers between devices, swap(): return lax.ppermute(value, AXES, xor_pairs(kind, flip))  43.6 us
    ppermute x18, starting transfers between devices, swap(): return lax.ppermute(value, AXES, xor_pairs(kind, flip))  35.4 us
    pallas_call x1, Pallas kernels, on_device(): pl.pallas_call(tile_kernel, out_shape=outs, in_specs=[pl.BlockSpec(memory...  13.5 us
    ppermute x4, starting transfers between devices, from_behind(): lax.ppermute(value, axis, [(source, source + steps) for source in range(f...  9.96 us
    pallas_call x4, Pallas kernels, call(): pl.pallas_call(kernel, out_shape=outs, in_specs=specs, out_specs=jax.tree...  3.81 us
    unnamed x29, local copies, waits for them, and re-layouts  3.03 us
  transfers between devices with their start and end apart: 22, of which 15 were waited for; matrix products, arithmetic and copies ran while one was open for 2% of the time, Pallas kernels for 0%

profile of v1, /device:TPU:6, one launch (start us, length us, event | category | flops | bytes accessed | tf_op | source)
XLA Modules:
  0.0 116.7 jit_solution(680874302077596725)
XLA Ops:
  1.3 1.3 %reshape.99.snd = s32[1,256]{1,0:T(1,128)} reshape(s32[1,1,8,32]{3,2,1,0:T(8,128)} %param.25) | data formatting | bytes 2048 | tf_op jit(solution)/shard_map/reshape | solution.py:339
  2.6 0.6 pad_add_fusion.place_ref
  3.2 13.5 %shard_map.183 = (bf16[2,96,512]{2,1,0:T(8,128)(2,1)}, bf16[2,96,512]{2,1,0:T(8,128)(2,1)}, bf16[2,32,512]{2,1,0:T(8,128)(2,1)}, bf16[2,32,512]{2,1,0:T(8,128)(2...) custom-call(s32[4]{0:T(128)} %pad_add_fusion.place_ref, s32[16,512]{1,0:T(8,128)} %bitcast.121, ...), custom_call_target="tpu_custom_call" | custom-call | tf_op jit(solution)/shard_map/pallas_call | solution.py:312
  16.8 1.3 %collective-permute-start = (bf16[2,96,512]{2,1,0:T(8,128)(2,1)}, bf16[2,96,512]{2,1,0:T(8,128)(2,1)S(1)}, u32[]{:S(2)}, u32[]{:S(2)}) collective-permute-start(bf16[2,96,512]{2,1,0:T(8,128)(2,1)} %get-tuple-element.24), channel_id=1, source_target_pairs={{8,0},{16,8},{24,16},{32,24},{40,32},{48,40},{56,48},{64,56},{72,6... | collective-permute-start | bytes 589832 | tf_op jit(solution)/shard_map/ppermute | solution.py:279
  18.1 1.2 %collective-permute-start.4 = (bf16[1040,512]{1,0:T(8,128)(2,1)}, bf16[1040,512]{1,0:T(8,128)(2,1)S(1)}, u32[]{:S(2)}, u32[]{:S(2)}) collective-permute-start(bf16[1040,512]{1,0:T(8,128)(2,1)} %get-tuple-element.29), channel_id=1, source_target_pairs={{0,8},{1,9},{2,10},{3,11},{4,12},{5,13},{6,14},{7,15},{8,0},{9,1},... | collective-permute-start | bytes 3194888 | tf_op jit(solution)/shard_map/ppermute | solution.py:54
  19.3 1.9 %collective-permute-start.1 = (bf16[2,96,512]{2,1,0:T(8,128)(2,1)}, bf16[2,96,512]{2,1,0:T(8,128)(2,1)S(1)}, u32[]{:S(2)}, u32[]{:S(2)}) collective-permute-start(bf16[2,96,512]{2,1,0:T(8,128)(2,1)} %get-tuple-element.25), channel_id=1, source_target_pairs={{0,8},{8,16},{16,24},{24,32},{32,40},{40,48},{48,56},{56,64},{64,7... | collective-permute-start | bytes 589832 | tf_op jit(solution)/shard_map/ppermute | solution.py:279
  21.2 0.0 collective-permute-done
  21.2 1.2 %collective-permute-done.1 = bf16[2,96,512]{2,1,0:T(8,128)(2,1)S(1)} collective-permute-done((bf16[2,96,512]{2,1,0:T(8,128)(2,1)}, bf16[2,96,512]{2,1,0:T(8,128)(2,1)S(1)}, u32[]{:S(2)}, u32[]{:S(2)}) %collective-permute-start.1) | collective-permute-done | bytes 196640 | tf_op jit(solution)/shard_map/ppermute | solution.py:279
  22.5 0.9 pad_maximum_fusion.2
  23.3 3.8 %collective-permute-start.3 = (bf16[2,3,32,512]{3,2,0,1:T(8,128)(2,1)S(1)}, bf16[2,3,32,512]{3,2,0,1:T(8,128)(2,1)S(1)}, u32[]{:S(2)}, u32[]{:S(2)}) collective-permute-start(bf16[2,3,32,512]{3,2,0,1:T(8,128)(2,1)S(1)} %pad_maximum_fusion.2), channel_id=1, source_target_pairs={{0,1},{1,2},{2,3},{3,4},{4,5},{5,6},{6,7},{8,9},{9,10},{10,11},{11... | collective-permute-start | bytes 589832 | tf_op jit(solution)/shard_map/ppermute | solution.py:279
  27.2 0.9 pad_maximum_fusion.1
  28.0 2.9 %collective-permute-start.2 = (bf16[2,3,32,512]{3,2,1,0:T(8,128)(2,1)S(1)}, bf16[2,3,32,512]{3,2,1,0:T(8,128)(2,1)S(1)}, u32[]{:S(2)}, u32[]{:S(2)}) collective-permute-start(bf16[2,3,32,512]{3,2,1,0:T(8,128)(2,1)S(1)} %pad_maximum_fusion.1), channel_id=1, source_target_pairs={{1,0},{2,1},{3,2},{4,3},{5,4},{6,5},{7,6},{9,8},{10,9},{11,10},{12... | collective-permute-start | bytes 589832 | tf_op jit(solution)/shard_map/ppermute | solution.py:279
  31.0 0.8 collective-permute-done.3
  31.8 0.0 collective-permute-done.4.refs_2_
  31.8 0.0 copy-start
  31.8 1.6 %copy-done = f32[1024,512]{1,0:T(8,128)S(1)} copy-done((f32[1024,512]{1,0:T(8,128)S(1)}, f32[1024,512]{1,0:T(8,128)}, u32[]{:S(2)}) %copy-start) | copy-done | bytes 2097176
  33.4 0.0 copy-start.1
  33.4 0.7 copy-done.1
  34.1 0.2 shard_map.184
  34.3 0.9 collective-permute-start.5
  35.2 1.1 collective-permute-start.6
  36.4 2.1 %collective-permute-start.7 = (bf16[272,512]{1,0:T(8,128)(2,1)S(1)}, bf16[272,512]{1,0:T(8,128)(2,1)S(1)}, u32[]{:S(2)}, u32[]{:S(2)}) collective-permute-start(bf16[272,512]{1,0:T(8,128)(2,1)S(1)} %get-tuple-element.34), channel_id=1, source_target_pairs={{0,4},{1,5},{2,6},{3,7},{4,0},{5,1},{6,2},{7,3},{8,136},{9,137},{1... | collective-permute-start | bytes 835592 | tf_op jit(solution)/shard_map/ppermute | solution.py:54
  38.5 0.0 collective-permute-done.2
  38.5 2.5 %collective-permute-done.5.refs_2_ = bf16[272,512]{1,0:T(8,128)(2,1)S(1)} collective-permute-done((bf16[272,512]{1,0:T(8,128)(2,1)S(1)}, bf16[272,512]{1,0:T(8,128)(2,1)S(1)}, u32[]{:S(2)}, u32[]{:S(2)}) %collective-permute-start.5) | collective-permute-done | bytes 278560 | tf_op jit(solution)/shard_map/ppermute | solution.py:54
  41.0 5.0 %collective-permute-done.6.refs_3_ = bf16[272,512]{1,0:T(8,128)(2,1)S(1)} collective-permute-done((bf16[272,512]{1,0:T(8,128)(2,1)S(1)}, bf16[272,512]{1,0:T(8,128)(2,1)S(1)}, u32[]{:S(2)}, u32[]{:S(2)}) %collective-permute-start.6) | collective-permute-done | bytes 278560 | tf_op jit(solution)/shard_map/ppermute | solution.py:54
  46.0 0.0 collective-permute-done.7.refs_4_
  46.0 0.1 shard_map.185
  46.1 17.2 %collective-permute-start.8 = (bf16[80,512]{1,0:T(8,128)(2,1)S(1)}, bf16[80,512]{1,0:T(8,128)(2,1)S(1)}, u32[]{:S(2)}, u32[]{:S(2)}) collective-permute-start(bf16[80,512]{1,0:T(8,128)(2,1)S(1)} %get-tuple-element.37), channel_id=1, source_target_pairs={{0,64},{1,65},{2,66},{3,67},{4,68},{5,69},{6,70},{7,71},{8,10},{9,... | collective-permute-start | bytes 245768 | tf_op jit(solution)/shard_map/ppermute | solution.py:54
  63.3 2.1 %collective-permute-start.9 = (bf16[80,512]{1,0:T(8,128)(2,1)S(1)}, bf16[80,512]{1,0:T(8,128)(2,1)S(1)}, u32[]{:S(2)}, u32[]{:S(2)}) collective-permute-start(bf16[80,512]{1,0:T(8,128)(2,1)S(1)} %get-tuple-element.38), channel_id=1, source_target_pairs={{0,192},{1,193},{2,194},{3,195},{4,196},{5,197},{6,198},{7,199},{8... | collective-permute-start | bytes 245768 | tf_op jit(solution)/shard_map/ppermute | solution.py:54
  65.4 1.0 collective-permute-start.10
  66.4 0.0 collective-permute-done.8.refs_2_
  66.4 2.5 %collective-permute-done.9.refs_3_ = bf16[80,512]{1,0:T(8,128)(2,1)S(1)} collective-permute-done((bf16[80,512]{1,0:T(8,128)(2,1)S(1)}, bf16[80,512]{1,0:T(8,128)(2,1)S(1)}, u32[]{:S(2)}, u32[]{:S(2)}) %collective-permute-start.9) | collective-permute-done | bytes 81952 | tf_op jit(solution)/shard_map/ppermute | solution.py:54
  69.0 2.4 %collective-permute-done.10.refs_4_ = bf16[80,512]{1,0:T(8,128)(2,1)S(1)} collective-permute-done((bf16[80,512]{1,0:T(8,128)(2,1)S(1)}, bf16[80,512]{1,0:T(8,128)(2,1)S(1)}, u32[]{:S(2)}, u32[]{:S(2)}) %collective-permute-start.10) | collective-permute-done | bytes 81952 | tf_op jit(solution)/shard_map/ppermute | solution.py:54
  71.4 0.7 collective-permute-start.11
  72.1 4.5 %collective-permute-done.11 = f32[72,512]{1,0:T(8,128)S(1)} collective-permute-done((f32[72,512]{1,0:T(8,128)S(1)}, f32[72,512]{1,0:T(8,128)S(1)}, u32[]{:S(2)}, u32[]{:S(2)}) %collective-permute-start.11) | collective-permute-done | bytes 147488 | tf_op jit(solution)/shard_map/ppermute | solution.py:54
  76.6 0.1 collective-permute-start.12
  76.8 0.0 copy-start.2
  76.8 6.9 %collective-permute-done.12 = f32[72,512]{1,0:T(8,128)S(1)} collective-permute-done((f32[72,512]{1,0:T(8,128)S(1)}, f32[72,512]{1,0:T(8,128)S(1)}, u32[]{:S(2)}, u32[]{:S(2)}) %collective-permute-start.12) | collective-permute-done | bytes 147488 | tf_op jit(solution)/shard_map/ppermute | solution.py:54
  83.7 0.9 collective-permute-start.13
  84.6 6.4 %collective-permute-done.13 = f32[72,512]{1,0:T(8,128)S(1)} collective-permute-done((f32[72,512]{1,0:T(8,128)S(1)}, f32[72,512]{1,0:T(8,128)S(1)}, u32[]{:S(2)}, u32[]{:S(2)}) %collective-permute-start.13) | collective-permute-done | bytes 147488 | tf_op jit(solution)/shard_map/ppermute | solution.py:54
  91.0 1.1 collective-permute-start.16
  92.1 2.6 %collective-permute-start.15 = (bf16[64,512]{1,0:T(8,128)(2,1)S(1)}, bf16[64,512]{1,0:T(8,128)(2,1)S(1)}, u32[]{:S(2)}, u32[]{:S(2)}) collective-permute-start(bf16[64,512]{1,0:T(8,128)(2,1)S(1)} %get-tuple-element.43), channel_id=1, source_target_pairs={{0,192},{1,193},{2,194},{3,195},{4,196},{5,197},{6,198},{7,199},{8... | collective-permute-start | bytes 196616 | tf_op jit(solution)/shard_map/ppermute | solution.py:54
  94.7 0.0 collective-permute-start.14
  94.7 2.1 %collective-permute-done.16 = bf16[64,512]{1,0:T(8,128)(2,1)S(1)} collective-permute-done((bf16[64,512]{1,0:T(8,128)(2,1)S(1)}, bf16[64,512]{1,0:T(8,128)(2,1)S(1)}, u32[]{:S(2)}, u32[]{:S(2)}) %collective-permute-start.16) | collective-permute-done | bytes 65568 | tf_op jit(solution)/shard_map/ppermute | solution.py:54
  96.8 0.7 collective-permute-done.15
  97.5 1.4 %collective-permute-done.14 = bf16[64,512]{1,0:T(8,128)(2,1)S(1)} collective-permute-done((bf16[64,512]{1,0:T(8,128)(2,1)S(1)}, bf16[64,512]{1,0:T(8,128)(2,1)S(1)}, u32[]{:S(2)}, u32[]{:S(2)}) %collective-permute-start.14) | collective-permute-done | bytes 65568 | tf_op jit(solution)/shard_map/ppermute | solution.py:54
  99.0 0.4 collective-permute-start.19
  99.4 2.2 %collective-permute-start.18 = (bf16[256,512]{1,0:T(8,128)(2,1)S(1)}, bf16[256,512]{1,0:T(8,128)(2,1)S(1)}, u32[]{:S(2)}, u32[]{:S(2)}) collective-permute-start(bf16[256,512]{1,0:T(8,128)(2,1)S(1)} %pad_maximum_fusion), channel_id=1, source_target_pairs={{0,6},{1,7},{2,4},{3,5},{4,2},{5,3},{6,0},{7,1},{8,200},{9,201},{1... | collective-permute-start | bytes 786440 | tf_op jit(solution)/shard_map/ppermute | solution.py:54
  101.6 1.0 collective-permute-start.17
  102.6 5.4 %collective-permute-done.17 = bf16[256,512]{1,0:T(8,128)(2,1)S(1)} collective-permute-done((bf16[256,512]{1,0:T(8,128)(2,1)S(1)}, bf16[256,512]{1,0:T(8,128)(2,1)S(1)}, u32[]{:S(2)}, u32[]{:S(2)}) %collective-permute-start.17) | collective-permute-done | bytes 262176 | tf_op jit(solution)/shard_map/ppermute | solution.py:54
  108.0 1.8 %collective-permute-done.18 = bf16[256,512]{1,0:T(8,128)(2,1)S(1)} collective-permute-done((bf16[256,512]{1,0:T(8,128)(2,1)S(1)}, bf16[256,512]{1,0:T(8,128)(2,1)S(1)}, u32[]{:S(2)}, u32[]{:S(2)}) %collective-permute-start.18) | collective-permute-done | bytes 262176 | tf_op jit(solution)/shard_map/ppermute | solution.py:54
  109.8 0.0 collective-permute-done.19
  109.8 0.1 collective-permute-start.20
  110.0 0.0 copy-start.3
  110.0 0.6 collective-permute-start.21
  110.6 0.0 copy-start.4
  110.6 2.0 %collective-permute-done.21.gate_other = f32[8,512]{1,0:T(8,128)S(1)} collective-permute-done((f32[8,512]{1,0:T(8,128)S(1)}, f32[8,512]{1,0:T(8,128)S(1)}, u32[]{:S(2)}, u32[]{:S(2)}) %collective-permute-start.21) | collective-permute-done | bytes 16416 | tf_op jit(solution)/shard_map/ppermute | solution.py:54
  112.6 0.0 collective-permute-done.20.other
  112.6 0.0 copy-done.2
  112.6 3.5 %shard_map.187 = (f32[2048,512]{1,0:T(8,128)}, f32[8,512]{1,0:T(8,128)S(1)}) custom-call(s32[4]{0:T(128)S(1)} %copy-done.2, bf16[1024,512]{1,0:T(8,128)(2,1)S(1)} %constant_dynamic-update-slice_fusion.16.own, bf16[1024,512]{1,0:T(8,128)(2,1)S(1)} %collective-permute-done.20.other, f32[8,512]{1,0:T(8,128)S(1)} %slice.154.gate_own, ...), custom_call_target="tpu_custom_call" | custom-call | tf_op jit(solution)/shard_map/pallas_call | solution.py:262
  116.1 0.6 copy.32
  116.7 0.0 copy-done.3
  116.7 0.0 copy-done.4
  (29 shorter events, 0.3 us)
Async XLA Ops:
  16.8 4.5 %collective-permute-start = (bf16[2,96,512]{2,1,0:T(8,128)(2,1)}, bf16[2,96,512]{2,1,0:T(8,128)(2,1)S(1)}, u32[]{:S(2)}, u32[]{:S(2)}) collective-permute-start(bf16[2,96,512]{2,1,0:T(8,128)(2,1)} %get-tuple-element.24), channel_id=1, source_target_pairs={{8,0},{16,8},{24,16},{32,24},{40,32},{48,40},{56,48},{64,56},{72,6... | collective-permute-start | bytes 589832 | tf_op jit(solution)/shard_map/ppermute | solution.py:279
  18.1 13.8 %collective-permute-start.4 = (bf16[1040,512]{1,0:T(8,128)(2,1)}, bf16[1040,512]{1,0:T(8,128)(2,1)S(1)}, u32[]{:S(2)}, u32[]{:S(2)}) collective-permute-start(bf16[1040,512]{1,0:T(8,128)(2,1)} %get-tuple-element.29), channel_id=1, source_target_pairs={{0,8},{1,9},{2,10},{3,11},{4,12},{5,13},{6,14},{7,15},{8,0},{9,1},... | collective-permute-start | bytes 3194888 | tf_op jit(solution)/shard_map/ppermute | solution.py:54
  19.3 3.2 %collective-permute-start.1 = (bf16[2,96,512]{2,1,0:T(8,128)(2,1)}, bf16[2,96,512]{2,1,0:T(8,128)(2,1)S(1)}, u32[]{:S(2)}, u32[]{:S(2)}) collective-permute-start(bf16[2,96,512]{2,1,0:T(8,128)(2,1)} %get-tuple-element.25), channel_id=1, source_target_pairs={{0,8},{8,16},{16,24},{24,32},{32,40},{40,48},{48,56},{56,64},{64,7... | collective-permute-start | bytes 589832 | tf_op jit(solution)/shard_map/ppermute | solution.py:279
  23.3 8.5 %collective-permute-start.3 = (bf16[2,3,32,512]{3,2,0,1:T(8,128)(2,1)S(1)}, bf16[2,3,32,512]{3,2,0,1:T(8,128)(2,1)S(1)}, u32[]{:S(2)}, u32[]{:S(2)}) collective-permute-start(bf16[2,3,32,512]{3,2,0,1:T(8,128)(2,1)S(1)} %pad_maximum_fusion.2), channel_id=1, source_target_pairs={{0,1},{1,2},{2,3},{3,4},{4,5},{5,6},{6,7},{8,9},{9,10},{10,11},{11... | collective-permute-start | bytes 589832 | tf_op jit(solution)/shard_map/ppermute | solution.py:279
  28.0 10.4 %collective-permute-start.2 = (bf16[2,3,32,512]{3,2,1,0:T(8,128)(2,1)S(1)}, bf16[2,3,32,512]{3,2,1,0:T(8,128)(2,1)S(1)}, u32[]{:S(2)}, u32[]{:S(2)}) collective-permute-start(bf16[2,3,32,512]{3,2,1,0:T(8,128)(2,1)S(1)} %pad_maximum_fusion.1), channel_id=1, source_target_pairs={{1,0},{2,1},{3,2},{4,3},{5,4},{6,5},{7,6},{9,8},{10,9},{11,10},{12... | collective-permute-start | bytes 589832 | tf_op jit(solution)/shard_map/ppermute | solution.py:279
  31.8 1.6 %copy-start = (f32[1024,512]{1,0:T(8,128)S(1)}, f32[1024,512]{1,0:T(8,128)}, u32[]{:S(2)}) copy-start(f32[1024,512]{1,0:T(8,128)} %get-tuple-element.27.refs_0_) | copy-start | bytes 6291460
  33.4 0.7 copy-start.1
  34.3 6.7 %collective-permute-start.5 = (bf16[272,512]{1,0:T(8,128)(2,1)S(1)}, bf16[272,512]{1,0:T(8,128)(2,1)S(1)}, u32[]{:S(2)}, u32[]{:S(2)}) collective-permute-start(bf16[272,512]{1,0:T(8,128)(2,1)S(1)} %get-tuple-element.32), channel_id=1, source_target_pairs={{0,2},{1,3},{2,0},{3,1},{4,6},{5,7},{6,4},{7,5},{8,72},{9,73},{10,... | collective-permute-start | bytes 835592 | tf_op jit(solution)/shard_map/ppermute | solution.py:54
  35.2 10.7 %collective-permute-start.6 = (bf16[272,512]{1,0:T(8,128)(2,1)S(1)}, bf16[272,512]{1,0:T(8,128)(2,1)S(1)}, u32[]{:S(2)}, u32[]{:S(2)}) collective-permute-start(bf16[272,512]{1,0:T(8,128)(2,1)S(1)} %get-tuple-element.33), channel_id=1, source_target_pairs={{0,6},{1,7},{2,4},{3,5},{4,2},{5,3},{6,0},{7,1},{8,200},{9,201},{1... | collective-permute-start | bytes 835592 | tf_op jit(solution)/shard_map/ppermute | solution.py:54
  36.4 9.6 %collective-permute-start.7 = (bf16[272,512]{1,0:T(8,128)(2,1)S(1)}, bf16[272,512]{1,0:T(8,128)(2,1)S(1)}, u32[]{:S(2)}, u32[]{:S(2)}) collective-permute-start(bf16[272,512]{1,0:T(8,128)(2,1)S(1)} %get-tuple-element.34), channel_id=1, source_target_pairs={{0,4},{1,5},{2,6},{3,7},{4,0},{5,1},{6,2},{7,3},{8,136},{9,137},{1... | collective-permute-start | bytes 835592 | tf_op jit(solution)/shard_map/ppermute | solution.py:54
  46.1 20.3 %collective-permute-start.8 = (bf16[80,512]{1,0:T(8,128)(2,1)S(1)}, bf16[80,512]{1,0:T(8,128)(2,1)S(1)}, u32[]{:S(2)}, u32[]{:S(2)}) collective-permute-start(bf16[80,512]{1,0:T(8,128)(2,1)S(1)} %get-tuple-element.37), channel_id=1, source_target_pairs={{0,64},{1,65},{2,66},{3,67},{4,68},{5,69},{6,70},{7,71},{8,10},{9,... | collective-permute-start | bytes 245768 | tf_op jit(solution)/shard_map/ppermute | solution.py:54
  63.3 5.7 %collective-permute-start.9 = (bf16[80,512]{1,0:T(8,128)(2,1)S(1)}, bf16[80,512]{1,0:T(8,128)(2,1)S(1)}, u32[]{:S(2)}, u32[]{:S(2)}) collective-permute-start(bf16[80,512]{1,0:T(8,128)(2,1)S(1)} %get-tuple-element.38), channel_id=1, source_target_pairs={{0,192},{1,193},{2,194},{3,195},{4,196},{5,197},{6,198},{7,199},{8... | collective-permute-start | bytes 245768 | tf_op jit(solution)/shard_map/ppermute | solution.py:54
  65.4 5.9 %collective-permute-start.10 = (bf16[80,512]{1,0:T(8,128)(2,1)S(1)}, bf16[80,512]{1,0:T(8,128)(2,1)S(1)}, u32[]{:S(2)}, u32[]{:S(2)}) collective-permute-start(bf16[80,512]{1,0:T(8,128)(2,1)S(1)} %get-tuple-element.39), channel_id=1, source_target_pairs={{0,128},{1,129},{2,130},{3,131},{4,132},{5,133},{6,134},{7,135},{8... | collective-permute-start | bytes 245768 | tf_op jit(solution)/shard_map/ppermute | solution.py:54
  71.4 5.2 %collective-permute-start.11 = (f32[72,512]{1,0:T(8,128)S(1)}, f32[72,512]{1,0:T(8,128)S(1)}, u32[]{:S(2)}, u32[]{:S(2)}) collective-permute-start(f32[72,512]{1,0:T(8,128)S(1)} %shard_map.186), channel_id=1, source_target_pairs={{0,1},{1,0},{2,3},{3,2},{4,5},{5,4},{6,7},{7,6},{8,9},{9,8},{10,11... | collective-permute-start | bytes 442376 | tf_op jit(solution)/shard_map/ppermute | solution.py:54
  76.6 7.0 %collective-permute-start.12 = (f32[72,512]{1,0:T(8,128)S(1)}, f32[72,512]{1,0:T(8,128)S(1)}, u32[]{:S(2)}, u32[]{:S(2)}) collective-permute-start(f32[72,512]{1,0:T(8,128)S(1)} %add.24), channel_id=1, source_target_pairs={{0,17},{1,16},{2,19},{3,18},{4,21},{5,20},{6,23},{7,22},{8,25},{9,... | collective-permute-start | bytes 442376 | tf_op jit(solution)/shard_map/ppermute | solution.py:54
  76.8 35.8 %copy-start.2 = (s32[4]{0:T(128)S(1)}, s32[4]{0:T(128)}, u32[]{:S(2)}) copy-start(s32[4]{0:T(128)} %pad_add_fusion.place_ref) | copy-start | bytes 52
  83.7 7.2 %collective-permute-start.13 = (f32[72,512]{1,0:T(8,128)S(1)}, f32[72,512]{1,0:T(8,128)S(1)}, u32[]{:S(2)}, u32[]{:S(2)}) collective-permute-start(f32[72,512]{1,0:T(8,128)S(1)} %add.25), channel_id=1, source_target_pairs={{0,49},{1,48},{2,51},{3,50},{4,53},{5,52},{6,55},{7,54},{8,57},{9,... | collective-permute-start | bytes 442376 | tf_op jit(solution)/shard_map/ppermute | solution.py:54
  91.0 5.9 %collective-permute-start.16 = (bf16[64,512]{1,0:T(8,128)(2,1)S(1)}, bf16[64,512]{1,0:T(8,128)(2,1)S(1)}, u32[]{:S(2)}, u32[]{:S(2)}) collective-permute-start(bf16[64,512]{1,0:T(8,128)(2,1)S(1)} %get-tuple-element.43), channel_id=1, source_target_pairs={{0,128},{1,129},{2,130},{3,131},{4,132},{5,133},{6,134},{7,135},{8... | collective-permute-start | bytes 196616 | tf_op jit(solution)/shard_map/ppermute | solution.py:54
  92.1 5.5 %collective-permute-start.15 = (bf16[64,512]{1,0:T(8,128)(2,1)S(1)}, bf16[64,512]{1,0:T(8,128)(2,1)S(1)}, u32[]{:S(2)}, u32[]{:S(2)}) collective-permute-start(bf16[64,512]{1,0:T(8,128)(2,1)S(1)} %get-tuple-element.43), channel_id=1, source_target_pairs={{0,192},{1,193},{2,194},{3,195},{4,196},{5,197},{6,198},{7,199},{8... | collective-permute-start | bytes 196616 | tf_op jit(solution)/shard_map/ppermute | solution.py:54
  94.7 4.3 %collective-permute-start.14 = (bf16[64,512]{1,0:T(8,128)(2,1)S(1)}, bf16[64,512]{1,0:T(8,128)(2,1)S(1)}, u32[]{:S(2)}, u32[]{:S(2)}) collective-permute-start(bf16[64,512]{1,0:T(8,128)(2,1)S(1)} %get-tuple-element.43), channel_id=1, source_target_pairs={{0,64},{1,65},{2,66},{3,67},{4,68},{5,69},{6,70},{7,71},{8,10},{9,... | collective-permute-start | bytes 196616 | tf_op jit(solution)/shard_map/ppermute | solution.py:54
  99.0 10.8 %collective-permute-start.19 = (bf16[256,512]{1,0:T(8,128)(2,1)S(1)}, bf16[256,512]{1,0:T(8,128)(2,1)S(1)}, u32[]{:S(2)}, u32[]{:S(2)}) collective-permute-start(bf16[256,512]{1,0:T(8,128)(2,1)S(1)} %pad_maximum_fusion), channel_id=1, source_target_pairs={{0,4},{1,5},{2,6},{3,7},{4,0},{5,1},{6,2},{7,3},{8,136},{9,137},{1... | collective-permute-start | bytes 786440 | tf_op jit(solution)/shard_map/ppermute | solution.py:54
  99.4 10.4 %collective-permute-start.18 = (bf16[256,512]{1,0:T(8,128)(2,1)S(1)}, bf16[256,512]{1,0:T(8,128)(2,1)S(1)}, u32[]{:S(2)}, u32[]{:S(2)}) collective-permute-start(bf16[256,512]{1,0:T(8,128)(2,1)S(1)} %pad_maximum_fusion), channel_id=1, source_target_pairs={{0,6},{1,7},{2,4},{3,5},{4,2},{5,3},{6,0},{7,1},{8,200},{9,201},{1... | collective-permute-start | bytes 786440 | tf_op jit(solution)/shard_map/ppermute | solution.py:54
  101.6 6.4 %collective-permute-start.17 = (bf16[256,512]{1,0:T(8,128)(2,1)S(1)}, bf16[256,512]{1,0:T(8,128)(2,1)S(1)}, u32[]{:S(2)}, u32[]{:S(2)}) collective-permute-start(bf16[256,512]{1,0:T(8,128)(2,1)S(1)} %pad_maximum_fusion), channel_id=1, source_target_pairs={{0,2},{1,3},{2,0},{3,1},{4,6},{5,7},{6,4},{7,5},{8,72},{9,73},{10,... | collective-permute-start | bytes 786440 | tf_op jit(solution)/shard_map/ppermute | solution.py:54
  109.8 2.8 %collective-permute-start.20 = (bf16[1024,512]{1,0:T(8,128)(2,1)S(1)}, bf16[1024,512]{1,0:T(8,128)(2,1)S(1)}, u32[]{:S(2)}, u32[]{:S(2)}) collective-permute-start(bf16[1024,512]{1,0:T(8,128)(2,1)S(1)} %constant_dynamic-update-slice_fusion.16.own), channel_id=1, source_target_pairs={{0,8},{1,9},{2,10},{3,11},{4,12},{5,13},{6,14},{7,15},{8,0},{9,1},... | collective-permute-start | bytes 3145736 | tf_op jit(solution)/shard_map/ppermute | solution.py:54
  110.0 6.7 %copy-start.3 = (bf16[256,512]{1,0:T(8,128)(2,1)}, bf16[256,512]{1,0:T(8,128)(2,1)S(1)}, u32[]{:S(2)}) copy-start(bf16[256,512]{1,0:T(8,128)(2,1)S(1)} %get-tuple-element.44) | copy-start | bytes 786436
  110.0 2.6 %collective-permute-start.21 = (f32[8,512]{1,0:T(8,128)S(1)}, f32[8,512]{1,0:T(8,128)S(1)}, u32[]{:S(2)}, u32[]{:S(2)}) collective-permute-start(f32[8,512]{1,0:T(8,128)S(1)} %slice.154.gate_own), channel_id=1, source_target_pairs={{0,8},{1,9},{2,10},{3,11},{4,12},{5,13},{6,14},{7,15},{8,0},{9,1},... | collective-permute-start | bytes 49160 | tf_op jit(solution)/shard_map/ppermute | solution.py:54
  110.6 6.1 %copy-start.4 = (bf16[256,512]{1,0:T(8,128)(2,1)}, bf16[256,512]{1,0:T(8,128)(2,1)S(1)}, u32[]{:S(2)}) copy-start(bf16[256,512]{1,0:T(8,128)(2,1)S(1)} %constant_dynamic-update-slice_fusion) | copy-start | bytes 786436

commit v2 on v1

v2 whole, which is shorter than its diff:
```python
import jax
import jax.numpy as jnp
from jax import lax
from jax.experimental import pallas as pl
from jax.experimental.pallas import tpu as pltpu
from jax.sharding import PartitionSpec as P

F32 = jnp.float32
BF16 = jnp.bfloat16
AXES = ("tx", "ty")


def ring_label(position):
    return position ^ (position >> 1)


def place(index):
    tx, ty = divmod(index, 8)
    y, z_hi, core = tx // 8, (tx // 2) % 4, tx % 2
    x, z_lo = ty // 2, ty % 2
    return x, y, z_hi * 2 + z_lo, core


def index_of(x, y, z, core):
    return (y * 8 + (z // 2) * 2 + core) * 8 + x * 2 + z % 2


def unlabel(label):
    return label ^ (label >> 1)


def xor_pairs(kind, flip):
    pairs = []
    for index in range(256):
        x, y, z, core = place(index)
        if kind == "core":
            core ^= 1
        elif kind == "z":
            label = (z ^ (z >> 1)) ^ flip
            z = label ^ (label >> 1) ^ (label >> 2)
        else:
            bit = core if kind == "first" else 1 - core
            x = unlabel(ring_label(x) ^ ((flip & 1) << bit))
            y = unlabel(ring_label(y) ^ ((flip >> 1) << bit))
        pairs.append((index, index_of(x, y, z, core)))
    return pairs


def swap(value, kind, flip=1):
    return lax.ppermute(value, AXES, xor_pairs(kind, flip))


def nn(a, b):
    return lax.dot_general(a, b, (((1,), (0,)), ((), ())), preferred_element_type=F32)


def nt(a, b):
    return lax.dot_general(a, b, (((1,), (1,)), ((), ())), preferred_element_type=F32)


def tn(a, b):
    return lax.dot_general(a, b, (((0,), (0,)), ((), ())), preferred_element_type=F32)


def my_labels():
    tx, ty = lax.axis_index("tx"), lax.axis_index("ty")
    x, y, core = ring_label(ty // 2), ring_label(tx // 8), tx % 2
    low = 2 * (y & 1) + (x & 1)
    high = 2 * (y >> 1) + (x >> 1)
    low_first, high_first = 4 * low + high, 4 * high + low
    mine = jnp.where(core == 0, low_first, high_first)
    partner = jnp.where(core == 0, high_first, low_first)
    return core, mine, partner


def put_gate(ref, row, gate):
    hi = gate.astype(BF16).astype(F32)
    lo = (gate - hi).astype(BF16).astype(F32)
    ref[row : row + 16, 0:128] = jnp.concatenate([hi, lo], 0).astype(BF16)
    return hi + lo


def get_gate(ref, row):
    both = ref[row : row + 16, 0:128].astype(F32)
    return both[0:8] + both[8:16]


def tile_kernel(
    live_ref, nbr_in, msk_in, snd_in, lig_in, rec_in, gwt_in,
    cells, halo, stale, sback, cot, expr, hexpr, ws, wn,
    o_lm, o_lp, o_mm, o_mp, o_keep, o_send, o_gate,
    full0, full1, xall, sb, ct, wsv, wnv, cnt, adj, slope_g, inner, slope0, agg0, grads,
    nbr, msk, snd, lig, rec, gwt, sems,
):
    n, w = ct.shape
    full_n = full0.shape[0]

    def fetch(src, dst, slot):
        copy = pltpu.make_async_copy(src, dst, sems.at[slot])
        copy.start()
        return copy

    small = (
        (nbr_in, nbr), (msk_in, msk), (lig_in, lig), (rec_in, rec), (gwt_in, gwt), (snd_in, snd),
    )
    c_small = [fetch(src, dst, 9 + k) for k, (src, dst) in enumerate(small)]
    c_expr = fetch(expr, xall.at[pl.ds(0, n)], 0)
    c_hexpr = fetch(hexpr, xall.at[pl.ds(n, full_n - n)], 1)
    c_cells = fetch(cells, full0.at[pl.ds(0, n)], 2)
    c_halo = fetch(halo, full0.at[pl.ds(n, full_n - n)], 3)
    c_ws = fetch(ws, wsv, 4)
    c_wn = fetch(wn, wnv, 5)
    c_stale = fetch(stale, full1.at[pl.ds(n, full_n - n)], 6)
    c_cot = fetch(cot, ct, 7)
    c_sb = fetch(sback, sb, 8)

    for copy in c_small:
        copy.wait()
    ids = nbr[...]
    low = jnp.bitwise_and(ids, 127)
    field = jnp.left_shift(msk[...], 5 * jnp.right_shift(ids, 7))
    rows128 = lax.broadcasted_iota(jnp.int32, (128, 128), 0)
    for part in range(n // 128):
        cols = slice(part * 128, part * 128 + 128)
        words = jnp.zeros((128, 128), jnp.int32)
        for k in range(ids.shape[0]):
            words = words + jnp.where(rows128 == low[k : k + 1, cols], field[k : k + 1, cols], 0)
        words = words.T
        for block in range(full_n // 128):
            count = jnp.bitwise_and(jnp.right_shift(words, 5 * block), 31)
            cnt[cols, block * 128 : block * 128 + 128] = (0.25 * count.astype(F32)).astype(BF16)

    genes = xall.shape[1]
    pairs = lig.shape[1]
    gene_rows = lax.broadcasted_iota(jnp.int32, (genes, pairs), 0)
    rec_table = jnp.where(gene_rows == rec[...], gwt[...], 0.0).astype(BF16)
    lig_table = jnp.where(gene_rows == lig[...], 1.0, 0.0).astype(BF16)
    mixed = nt(rec_table, lig_table).astype(BF16)
    c_expr.wait()
    c_hexpr.wait()
    left = nn(xall[0:n], mixed).astype(BF16)
    half_tanh = 0.5 * jnp.tanh(0.5 * nt(left, xall[...]))
    count = cnt[...].astype(F32)
    weight = count * (0.5 + half_tanh)
    adj[...] = weight.astype(BF16)
    slope_g[...] = weight * (0.5 - half_tanh)

    c_cells.wait()
    c_halo.wait()
    state0 = full0[0:n]
    agg0[...] = nn(adj[...], full0[...]).astype(BF16)
    c_ws.wait()
    c_wn.wait()
    pre0 = nn(state0, wsv[0]) + nn(agg0[...], wnv[0])
    sig0 = 0.5 + 0.5 * jnp.tanh(0.5 * pre0)
    slope0[...] = sig0 * (1.0 + pre0 * (1.0 - sig0))
    full1[0:n] = (state0.astype(F32) + pre0 * sig0).astype(BF16)

    c_stale.wait()
    agg1 = nn(adj[...], full1[...]).astype(BF16)
    pre1 = nn(full1[0:n], wsv[1]) + nn(agg1, wnv[1])
    sig1 = 0.5 + 0.5 * jnp.tanh(0.5 * pre1)
    slope1 = sig1 * (1.0 + pre1 * (1.0 - sig1))
    c_cot.wait()
    live = lax.broadcasted_iota(jnp.int32, (n, w), 0) < live_ref[0, 0]
    carried = jnp.where(live, ct[...].astype(F32), 0.0)
    gpre1 = (carried * slope1).astype(BF16)
    grads[2 * n : 3 * n] = tn(full1[0:n], gpre1)
    grads[3 * n : 4 * n] = tn(agg1, gpre1)
    gagg1 = nt(gpre1, wnv[1]).astype(BF16)
    inner[...] = nt(gagg1, full1[...])
    gfull = tn(adj[...], gagg1)
    back = gfull[n:].astype(BF16)

    send_ids = jnp.concatenate([snd[d : d + 1] for d in range(8)], axis=1)
    sent = send_ids.shape[1]
    send_table = jnp.where(
        lax.broadcasted_iota(jnp.int32, (n, sent), 0) == send_ids, 1.0, 0.0
    ).astype(BF16)
    fresh = tn(send_table, full1[0:n]).astype(BF16)
    b = sent // 8
    o_lm[0] = fresh[0 : 3 * b]
    o_lp[0] = fresh[5 * b : 8 * b]
    o_mm[0] = fresh[3 * b : 4 * b]
    o_mp[0] = fresh[4 * b : 5 * b]
    for pos in range(3):
        o_lm[1, pos * b : (pos + 1) * b] = back[(7 - pos) * b : (8 - pos) * b]
        o_lp[1, pos * b : (pos + 1) * b] = back[(2 - pos) * b : (3 - pos) * b]
    o_mm[1] = back[4 * b : 5 * b]
    o_mp[1] = back[3 * b : 4 * b]

    c_sb.wait()
    carried = carried + nt(gpre1, wsv[1]) + gfull[:n] + nn(send_table, sb[...])
    gpre0 = (carried * slope0[...]).astype(BF16)
    grads[0:n] = tn(state0, gpre0)
    grads[n : 2 * n] = tn(agg0[...], gpre0)
    gagg0 = nt(gpre0, wnv[0]).astype(BF16)
    spread = (slope_g[...] * (inner[...] + nt(gagg0, full0[...]))).astype(BF16)
    gathered = nn(spread, xall[...]).astype(BF16)
    gene_grad = tn(xall[0:n], gathered)
    gene_hi = gene_grad.astype(BF16)
    gene_lo = (gene_grad - gene_hi.astype(F32)).astype(BF16)
    by_pair = nn(gene_hi, lig_table) + nn(gene_lo, lig_table)
    gate = jnp.sum(jnp.where(gene_rows == rec[...], by_pair, 0.0), axis=0, keepdims=True)
    gate = jnp.concatenate([gate[:, k * 128 : k * 128 + 128] for k in range(8)], axis=0)

    core, mine, partner = my_labels()
    half = 2 * n
    step = half // 16
    for j in range(16):
        here = pl.multiple_of(core * half + (mine ^ j) * step, step)
        there = pl.multiple_of((1 - core) * half + (partner ^ j) * step, step)
        o_keep[j * step : (j + 1) * step] = grads[pl.ds(here, step)]
        o_send[j * step : (j + 1) * step] = grads[pl.ds(there, step)].astype(BF16)
    o_gate[...] = put_gate(o_send, half, gate)


def split_four(total, gates, rows, keep, gate_out, sends):
    part = rows // 4
    keep[...] = total(0, part)
    for j, ref in enumerate(sends, 1):
        ref[0:part] = total(j * part, (j + 1) * part).astype(BF16)
        kept = put_gate(ref, part, gates)
    gate_out[...] = kept


def after_core(own, gate, got, lead_m, lead_p, keep, gate_out, s1, s2, s3, o_lm, o_lp):
    rows = own.shape[0]
    split_four(
        lambda lo, hi: own[lo:hi] + got[lo:hi].astype(F32),
        gate[...] + get_gate(got, rows),
        rows, keep, gate_out, (s1, s2, s3),
    )
    o_lm[...] = lead_m[...]
    o_lp[...] = lead_p[...]


def four(own, got):
    def total(lo, hi):
        return (own[lo:hi] + got[2][lo:hi].astype(F32)) + (
            got[0][lo:hi].astype(F32) + got[1][lo:hi].astype(F32)
        )

    return total


def four_gates(gate, got, rows):
    return (gate[...] + get_gate(got[2], rows)) + (get_gate(got[0], rows) + get_gate(got[1], rows))


def after_first(
    own, gate, r1, r2, r3, lead_m, lead_p, mid_m, mid_p,
    keep, gate_out, s1, s2, s3, cross_m, cross_p,
):
    rows = own.shape[0]
    got = (r1, r2, r3)
    split_four(four(own, got), four_gates(gate, got, rows), rows, keep, gate_out, (s1, s2, s3))
    b = mid_m.shape[1]
    for k in range(2):
        for ref, mid, cut in ((cross_m, mid_m, 0), (cross_p, mid_p, 2)):
            ref[k, 0:b] = mid[k]
            ref[k, b : 2 * b] = lead_m[k, cut * b : (cut + 1) * b]
            ref[k, 2 * b : 3 * b] = lead_p[k, cut * b : (cut + 1) * b]


def after_second(own, gate, r1, r2, r3, out):
    rows = own.shape[0]
    got = (r1, r2, r3)
    out[0:rows] = four(own, got)(0, rows)
    out[rows:, 0:128] = four_gates(gate, got, rows)


def add_wide(a, b, out):
    rows = out.shape[0] - 16
    out[0:rows] = (a[0:rows] + b[0:rows]).astype(BF16)
    put_gate(out, rows, a[rows:, 0:128] + b[rows:, 0:128])


def add_narrow(a, b, out):
    rows = out.shape[0] - 16
    out[0:rows] = (a[0:rows].astype(F32) + b[0:rows].astype(F32)).astype(BF16)
    put_gate(out, rows, get_gate(a, rows) + get_gate(b, rows))


def add_last(a, b, own, gate):
    rows = own.shape[0]
    own[...] = (a[0:rows].astype(F32) + b[0:rows].astype(F32)).astype(BF16)
    put_gate(gate, 0, get_gate(a, rows) + get_gate(b, rows))


def join(*refs):
    out, row = refs[-1], 0
    for ref in refs[:-1]:
        out[row : row + ref.shape[0]] = ref[...]
        row += ref.shape[0]


def join_through(own, r1, r2, r3, gate, cross_m, cross_p, out, o_cross_m, o_cross_p):
    join(own, r1, r2, r3, gate, out)
    o_cross_m[...] = cross_m[...]
    o_cross_p[...] = cross_p[...]


def squares(ref, label):
    rows, w = ref.shape[0] - 16, ref.shape[1]
    step = rows // 16
    total = jnp.zeros((8, w), F32)
    for j in range(16):
        part = ref[pl.ds(pl.multiple_of((label ^ j) * step, step), step)].astype(F32)
        part = part * part
        for k in range(step // 8):
            total = total + part[k * 8 : (k + 1) * 8]
    return total


def own_squares(own, lead_m, lead_p, cross_m, cross_p, o_squares, o_fresh, o_returned):
    _, mine, _ = my_labels()
    o_squares[...] = squares(own, mine)
    b = o_fresh.shape[0] // 8
    arrived = (
        (cross_m, 1), (lead_m, 1), (cross_p, 1), (cross_m, 0),
        (cross_p, 0), (cross_m, 2), (lead_p, 1), (cross_p, 2),
    )
    for d, (ref, cut) in enumerate(arrived):
        o_fresh[d * b : (d + 1) * b] = ref[0, cut * b : (cut + 1) * b]
        o_returned[(7 - d) * b : (8 - d) * b] = ref[1, cut * b : (cut + 1) * b]


def last_kernel(own, other, own_sq, o_layers, o_gate, whole, sems):
    rows, w = own.shape[0] - 16, own.shape[1]
    core, mine, partner = my_labels()
    step = rows // 16
    other_sq = squares(other, partner)
    gate = jnp.where(core == 0, get_gate(own, rows), get_gate(other, rows))
    total = jnp.sum(own_sq[...] + other_sq, axis=0, keepdims=True)
    square = jnp.sum(total, axis=1, keepdims=True)
    square = square + jnp.sum(
        jnp.sum(gate * gate, axis=0, keepdims=True), axis=1, keepdims=True
    )
    clip = jnp.minimum(1.0, (2.0 * w) / jnp.sqrt(square + 1e-06))
    o_gate[...] = gate * clip
    copies = []
    for side, (ref, label, which) in enumerate(((own, mine, core), (other, partner, 1 - core))):
        for group in range(4):
            slot = side * 4 + group
            for j in range(4 * group, 4 * group + 4):
                row = pl.multiple_of((label ^ j) * step, step)
                part = ref[pl.ds(row, step)].astype(F32) * clip
                whole[side * rows + j * step : side * rows + (j + 1) * step] = part
            target = pl.multiple_of(which * rows + group * 4 * step, step)
            copy = pltpu.make_async_copy(
                whole.at[pl.ds(side * rows + group * 4 * step, 4 * step)],
                o_layers.at[pl.ds(target, 4 * step)],
                sems.at[slot],
            )
            copy.start()
            copies.append(copy)
    for copy in copies:
        copy.wait()


def call(kernel, outs, *args, scratch=(), hbm_outs=0):
    vmem, hbm = pl.BlockSpec(memory_space=pltpu.VMEM), pl.BlockSpec(memory_space=pl.ANY)
    return pl.pallas_call(
        kernel,
        out_shape=outs,
        in_specs=[vmem] * len(args),
        out_specs=(hbm,) * hbm_outs + (vmem,) * (len(outs) - hbm_outs),
        scratch_shapes=list(scratch),
        compiler_params=pltpu.CompilerParams(vmem_limit_bytes=16 * 1024 * 1024),
    )(*args)


def shape(rows, w, kind):
    return jax.ShapeDtypeStruct((rows, w), kind)


def from_behind(value, axis, steps):
    count = lax.axis_size(axis)
    first, last = (max(0, -steps), min(count, count - steps))
    return lax.ppermute(value, axis, [(source, source + steps) for source in range(first, last)])


def on_device(
    cells, halo_inputs, stale_halo, stale_returned, cotangent, expression, halo_expression,
    neighbours, edge_mask, send_rows, live_cells, ligand_genes, receptor_genes, gate_weights,
    self_weights, neighbour_weights,
):
    n, w = cells.shape[2:]
    h = halo_inputs.shape[2]
    degree = neighbours.shape[2]
    pairs = ligand_genes.shape[0]
    genes = expression.shape[3]
    b = h // 8

    vmem = pl.BlockSpec(memory_space=pltpu.VMEM)
    hbm = pl.BlockSpec(memory_space=pltpu.HBM)
    outs = (
        jax.ShapeDtypeStruct((2, 3 * b, w), BF16),
        jax.ShapeDtypeStruct((2, 3 * b, w), BF16),
        jax.ShapeDtypeStruct((2, b, w), BF16),
        jax.ShapeDtypeStruct((2, b, w), BF16),
        shape(2 * n, w, F32),
        shape(2 * n + 16, w, BF16),
        shape(8, 128, F32),
    )
    lead_m, lead_p, mid_m, mid_p, keep, send, gate = pl.pallas_call(
        tile_kernel,
        out_shape=outs,
        in_specs=[pl.BlockSpec(memory_space=pltpu.SMEM)] + [hbm] * 15,
        out_specs=(vmem,) * len(outs),
        scratch_shapes=[
            pltpu.VMEM((n + h, w), BF16),
            pltpu.VMEM((n + h, w), BF16),
            pltpu.VMEM((n + h, genes), BF16),
            pltpu.VMEM((h, w), BF16),
            pltpu.VMEM((n, w), BF16),
            pltpu.VMEM((2, w, w), BF16),
            pltpu.VMEM((2, w, w), BF16),
            pltpu.VMEM((n, n + h), BF16),
            pltpu.VMEM((n, n + h), BF16),
            pltpu.VMEM((n, n + h), F32),
            pltpu.VMEM((n, n + h), F32),
            pltpu.VMEM((n, w), F32),
            pltpu.VMEM((n, w), BF16),
            pltpu.VMEM((4 * n, w), F32),
            pltpu.VMEM((degree, n), jnp.int32),
            pltpu.VMEM((degree, n), jnp.int32),
            pltpu.VMEM((8, b), jnp.int32),
            pltpu.VMEM((1, pairs), jnp.int32),
            pltpu.VMEM((1, pairs), jnp.int32),
            pltpu.VMEM((1, pairs), F32),
            pltpu.SemaphoreType.DMA((15,)),
        ],
        compiler_params=pltpu.CompilerParams(vmem_limit_bytes=40 * 1024 * 1024),
    )(
        live_cells,
        *(
            pltpu.with_memory_space_constraint(value, pltpu.HBM)
            for value in (
                neighbours.reshape(degree, n),
                edge_mask.reshape(degree, n),
                send_rows.reshape(8, b),
                ligand_genes.reshape(1, pairs),
                receptor_genes.reshape(1, pairs),
                gate_weights.reshape(1, pairs),
                cells.reshape(n, w),
                halo_inputs.reshape(h, w),
                stale_halo.reshape(h, w),
                stale_returned.reshape(h, w),
                cotangent.reshape(n, w),
                expression.reshape(n, genes),
                halo_expression.reshape(h, genes),
                self_weights,
                neighbour_weights,
            )
        ),
    )

    def quarter(part):
        return (shape(part, w, F32), shape(8, 128, F32)) + (shape(part + 16, w, BF16),) * 3

    wide = jax.ShapeDtypeStruct((2, 3 * b, w), BF16)
    got = swap(send, "core")
    part = n // 2
    keep, gate, s1, s2, s3, lead_m, lead_p = call(
        after_core, quarter(part) + (wide, wide), keep, gate, got, lead_m, lead_p
    )
    got = [swap(value, "first", j) for j, value in ((1, s1), (2, s2), (3, s3))]
    lead_m = from_behind(lead_m, "tx", -1)
    lead_p = from_behind(lead_p, "tx", 1)
    part = part // 4
    keep, gate, s1, s2, s3, cross_m, cross_p = call(
        after_first, quarter(part) + (wide, wide), keep, gate, *got, lead_m, lead_p, mid_m, mid_p
    )
    got = [swap(value, "second", j) for j, value in ((1, s1), (2, s2), (3, s3))]
    (both,) = call(after_second, (shape(part + 8, w, F32),), keep, gate, *got)
    (both,) = call(add_wide, (shape(part + 16, w, BF16),), both, swap(both, "z", 1))
    (both,) = call(add_narrow, (shape(part + 16, w, BF16),), both, swap(both, "z", 2))
    own, gate = call(
        add_last, (shape(part, w, BF16), shape(16, w, BF16)), both, swap(both, "z", 4)
    )
    got = [swap(own, "second", j) for j in (1, 2, 3)]
    (own,) = call(join, (shape(4 * part, w, BF16),), own, *got)
    got = [swap(own, "first", j) for j in (1, 2, 3)]
    cross_m = from_behind(cross_m, "ty", -1)
    cross_p = from_behind(cross_p, "ty", 1)
    own, cross_m, cross_p = call(
        join_through, (shape(16 * part + 16, w, BF16), wide, wide), own, *got, gate, cross_m, cross_p
    )
    other = swap(own, "core")
    own_sq, fresh, returned = call(
        own_squares, (shape(8, w, F32), shape(h, w, BF16), shape(h, w, BF16)),
        own, lead_m, lead_p, cross_m, cross_p,
    )
    layers, gate = call(
        last_kernel, (shape(4 * n, w, F32), shape(8, 128, F32)), own, other, own_sq,
        scratch=[pltpu.VMEM((4 * n, w), F32), pltpu.SemaphoreType.DMA((8,))], hbm_outs=1,
    )
    halo_shape = (1, 1, 1, h, w)
    return (
        fresh.reshape(halo_shape),
        returned.reshape(halo_shape),
        layers.reshape(4, n, w),
        gate.reshape(pairs),
    )


def solution(mesh):
    tile = P("tx", "ty")
    return jax.shard_map(
        on_device,
        mesh=mesh,
        in_specs=(tile,) * 11 + (P(),) * 5,
        out_specs=(tile, tile, P(), P()),
        check_vma=False,
    )
```

time: 119 us -> 103 us (0.87); the launches traced: 117 us -> 102 us
  waiting for transfers between devices: 45.6 us -> 38 us
  local copies, waits for them, and re-layouts: 4.41 us -> 0 us
  other arithmetic: 2.41 us -> 0 us
    ppermute x18 -> x17, waiting for transfers between devices: 43.6 us -> 30.6 us  [swap(): return lax.ppermute(value, AXES, xor_pairs(kind, flip))]
    ppermute x4, waiting for transfers between devices: 2.06 us -> 7.47 us  [from_behind(): lax.ppermute(value, axis, [(source, source + steps) for source in range(f...]
    unnamed x29 -> x0, local copies, waits for them, and re-layouts: 3.03 us -> none
    another operation x3 -> x0, other arithmetic: 2.32 us -> none  [the longest x1 0.87 us: on_device(): cross_m = jnp.stack([mid_m, lead_m[:, 0], lead_p[:, 0]], 1)]
    ppermute x4, starting transfers between devices: 9.96 us -> 11.4 us  [from_behind(): lax.ppermute(value, axis, [(source, source + steps) for source in range(f...]
    reshape x1 -> x0, local copies, waits for them, and re-layouts: 1.33 us -> none  [on_device(): send_rows.reshape(1, h)]
    ppermute x18 -> x17, starting transfers between devices: 35.4 us -> 34.2 us  [swap(): return lax.ppermute(value, AXES, xor_pairs(kind, flip))]
    pallas_call x4 -> x10, Pallas kernels: 3.81 us -> 4.3 us  [call(): pl.pallas_call(kernel, out_shape=outs, in_specs=[vmem] * len(args), out_s...]
  transfers between devices with their start and end apart: 22 -> 21, of which waited for: 15 -> 14; matrix products, arithmetic and copies ran while one was open for 2% -> 0% of each run, Pallas kernels for 0% -> 1%
where the time goes in v2:
time: 103 us; the launch traced here: 102 us
  starting transfers between devices  45.7 us (44%)
  waiting for transfers between devices  38 us (37%)
  Pallas kernels  17.1 us (17%)
  between operations  1.57 us (2%)
    ppermute x17, starting transfers between devices, swap(): return lax.ppermute(value, AXES, xor_pairs(kind, flip))  34.2 us
    ppermute x17, waiting for transfers between devices, swap(): return lax.ppermute(value, AXES, xor_pairs(kind, flip))  30.6 us
    pallas_call x1, Pallas kernels, on_device(): pl.pallas_call(tile_kernel, out_shape=outs, in_specs=[pl.BlockSpec(memory...  12.8 us
    ppermute x4, starting transfers between devices, from_behind(): lax.ppermute(value, axis, [(source, source + steps) for source in range(f...  11.4 us
    ppermute x4, waiting for transfers between devices, from_behind(): lax.ppermute(value, axis, [(source, source + steps) for source in range(f...  7.47 us
    pallas_call x10, Pallas kernels, call(): pl.pallas_call(kernel, out_shape=outs, in_specs=[vmem] * len(args), out_s...  4.3 us
  transfers between devices with their start and end apart: 21, of which 14 were waited for; matrix products, arithmetic and copies ran while one was open for 0% of the time, Pallas kernels for 1%

profile of v2, /device:TPU:6, one launch (start us, length us, event | category | flops | bytes accessed | tf_op | source)
XLA Modules:
  0.0 102.3 jit_solution(16501295736361967475)
XLA Ops:
  1.3 12.8 %shard_map.183 = (bf16[2,96,512]{2,1,0:T(8,128)(2,1)S(1)}, bf16[2,96,512]{2,1,0:T(8,128)(2,1)S(1)}, bf16[2,32,512]{2,1,0:T(8,128)(2,1)S(1)}, bf16[2,32,512]{2,1,...) custom-call(s32[1,1]{1,0:T(1,128)S(6)} %copy.20.live_ref, ...), custom_call_target="tpu_custom_call" | custom-call | tf_op jit(solution)/shard_map/pallas_call | solution.py:407
  14.0 0.1 collective-permute-start
  14.2 2.7 %collective-permute-done.got = bf16[1040,512]{1,0:T(8,128)(2,1)S(1)} collective-permute-done((bf16[1040,512]{1,0:T(8,128)(2,1)S(1)}, bf16[1040,512]{1,0:T(8,128)(2,1)S(1)}, u32[]{:S(2)}, u32[]{:S(2)}) %collective-permute-start) | collective-permute-done | bytes 1064992 | tf_op jit(solution)/shard_map/ppermute | solution.py:50
  16.8 0.2 shard_map.184
  17.0 0.9 collective-permute-start.1
  17.9 1.6 %collective-permute-start.2 = (bf16[272,512]{1,0:T(8,128)(2,1)S(1)}, bf16[272,512]{1,0:T(8,128)(2,1)S(1)}, u32[]{:S(2)}, u32[]{:S(2)}) collective-permute-start(bf16[272,512]{1,0:T(8,128)(2,1)S(1)} %get-tuple-element.43), channel_id=1, source_target_pairs={{0,64},{1,65},{2,66},{3,67},{4,68},{5,69},{6,70},{7,71},{8,200},{9... | collective-permute-start | bytes 835592 | tf_op jit(solution)/shard_map/ppermute | solution.py:50
  19.5 1.1 %collective-permute-start.3 = (bf16[272,512]{1,0:T(8,128)(2,1)S(1)}, bf16[272,512]{1,0:T(8,128)(2,1)S(1)}, u32[]{:S(2)}, u32[]{:S(2)}) collective-permute-start(bf16[272,512]{1,0:T(8,128)(2,1)S(1)} %get-tuple-element.44), channel_id=1, source_target_pairs={{0,66},{1,67},{2,64},{3,65},{4,70},{5,71},{6,68},{7,69},{8,206},{9... | collective-permute-start | bytes 835592 | tf_op jit(solution)/shard_map/ppermute | solution.py:50
  20.6 1.3 %collective-permute-start.4 = (bf16[2,96,512]{2,1,0:T(8,128)(2,1)S(1)}, bf16[2,96,512]{2,1,0:T(8,128)(2,1)S(1)}, u32[]{:S(2)}, u32[]{:S(2)}) collective-permute-start(bf16[2,96,512]{2,1,0:T(8,128)(2,1)S(1)} %get-tuple-element.45), channel_id=1, source_target_pairs={{8,0},{16,8},{24,16},{32,24},{40,32},{48,40},{56,48},{64,56},{72,6... | collective-permute-start | bytes 589832 | tf_op jit(solution)/shard_map/ppermute | solution.py:381
  21.9 4.3 %collective-permute-start.5 = (bf16[2,96,512]{2,1,0:T(8,128)(2,1)S(1)}, bf16[2,96,512]{2,1,0:T(8,128)(2,1)S(1)}, u32[]{:S(2)}, u32[]{:S(2)}) collective-permute-start(bf16[2,96,512]{2,1,0:T(8,128)(2,1)S(1)} %get-tuple-element.46), channel_id=1, source_target_pairs={{0,8},{8,16},{16,24},{24,32},{32,40},{40,48},{48,56},{56,64},{64,7... | collective-permute-start | bytes 589832 | tf_op jit(solution)/shard_map/ppermute | solution.py:381
  26.2 0.0 collective-permute-done.4.lead_m
  26.2 1.0 %collective-permute-done.5.lead_p = bf16[2,96,512]{2,1,0:T(8,128)(2,1)S(1)} collective-permute-done((bf16[2,96,512]{2,1,0:T(8,128)(2,1)S(1)}, bf16[2,96,512]{2,1,0:T(8,128)(2,1)S(1)}, u32[]{:S(2)}, u32[]{:S(2)}) %collective-permute-start.5) | collective-permute-done | bytes 196640 | tf_op jit(solution)/shard_map/ppermute | solution.py:381
  27.3 0.0 collective-permute-done.1.r1
  27.3 0.0 collective-permute-done.2.r2
  27.3 0.4 collective-permute-done.3.r3
  27.6 0.2 shard_map.185
  27.8 1.8 %collective-permute-start.6 = (bf16[80,512]{1,0:T(8,128)(2,1)S(1)}, bf16[80,512]{1,0:T(8,128)(2,1)S(1)}, u32[]{:S(2)}, u32[]{:S(2)}) collective-permute-start(bf16[80,512]{1,0:T(8,128)(2,1)S(1)} %get-tuple-element.51), channel_id=1, source_target_pairs={{0,6},{1,7},{2,4},{3,5},{4,2},{5,3},{6,0},{7,1},{8,10},{9,11},{10,... | collective-permute-start | bytes 245768 | tf_op jit(solution)/shard_map/ppermute | solution.py:50
  29.6 14.6 %collective-permute-start.7 = (bf16[80,512]{1,0:T(8,128)(2,1)S(1)}, bf16[80,512]{1,0:T(8,128)(2,1)S(1)}, u32[]{:S(2)}, u32[]{:S(2)}) collective-permute-start(bf16[80,512]{1,0:T(8,128)(2,1)S(1)} %get-tuple-element.52), channel_id=1, source_target_pairs={{0,192},{1,193},{2,194},{3,195},{4,196},{5,197},{6,198},{7,199},{8... | collective-permute-start | bytes 245768 | tf_op jit(solution)/shard_map/ppermute | solution.py:50
  44.2 2.2 %collective-permute-start.8 = (bf16[80,512]{1,0:T(8,128)(2,1)S(1)}, bf16[80,512]{1,0:T(8,128)(2,1)S(1)}, u32[]{:S(2)}, u32[]{:S(2)}) collective-permute-start(bf16[80,512]{1,0:T(8,128)(2,1)S(1)} %get-tuple-element.53), channel_id=1, source_target_pairs={{0,198},{1,199},{2,196},{3,197},{4,194},{5,195},{6,192},{7,193},{8... | collective-permute-start | bytes 245768 | tf_op jit(solution)/shard_map/ppermute | solution.py:50
  46.5 0.0 collective-permute-done.6.r1
  46.5 0.2 collective-permute-done.7.r2
  46.6 5.3 %collective-permute-done.8.r3 = bf16[80,512]{1,0:T(8,128)(2,1)S(1)} collective-permute-done((bf16[80,512]{1,0:T(8,128)(2,1)S(1)}, bf16[80,512]{1,0:T(8,128)(2,1)S(1)}, u32[]{:S(2)}, u32[]{:S(2)}) %collective-permute-start.8) | collective-permute-done | bytes 81952 | tf_op jit(solution)/shard_map/ppermute | solution.py:50
  52.0 1.8 %collective-permute-start.9 = (f32[72,512]{1,0:T(8,128)S(1)}, f32[72,512]{1,0:T(8,128)S(1)}, u32[]{:S(2)}, u32[]{:S(2)}) collective-permute-start(f32[72,512]{1,0:T(8,128)S(1)} %shard_map.186.a), channel_id=1, source_target_pairs={{0,1},{1,0},{2,3},{3,2},{4,5},{5,4},{6,7},{7,6},{8,9},{9,8},{10,11... | collective-permute-start | bytes 442376 | tf_op jit(solution)/shard_map/ppermute | solution.py:50
  53.8 4.2 %collective-permute-done.9.b = f32[72,512]{1,0:T(8,128)S(1)} collective-permute-done((f32[72,512]{1,0:T(8,128)S(1)}, f32[72,512]{1,0:T(8,128)S(1)}, u32[]{:S(2)}, u32[]{:S(2)}) %collective-permute-start.9) | collective-permute-done | bytes 147488 | tf_op jit(solution)/shard_map/ppermute | solution.py:50
  58.1 0.1 collective-permute-start.10
  58.2 6.2 %collective-permute-done.10.b = bf16[80,512]{1,0:T(8,128)(2,1)S(1)} collective-permute-done((bf16[80,512]{1,0:T(8,128)(2,1)S(1)}, bf16[80,512]{1,0:T(8,128)(2,1)S(1)}, u32[]{:S(2)}, u32[]{:S(2)}) %collective-permute-start.10) | collective-permute-done | bytes 81952 | tf_op jit(solution)/shard_map/ppermute | solution.py:50
  64.5 0.3 collective-permute-start.11
  64.8 6.2 %collective-permute-done.11.b = bf16[80,512]{1,0:T(8,128)(2,1)S(1)} collective-permute-done((bf16[80,512]{1,0:T(8,128)(2,1)S(1)}, bf16[80,512]{1,0:T(8,128)(2,1)S(1)}, u32[]{:S(2)}, u32[]{:S(2)}) %collective-permute-start.11) | collective-permute-done | bytes 81952 | tf_op jit(solution)/shard_map/ppermute | solution.py:50
  71.1 2.4 %collective-permute-start.14 = (bf16[64,512]{1,0:T(8,128)(2,1)S(1)}, bf16[64,512]{1,0:T(8,128)(2,1)S(1)}, u32[]{:S(2)}, u32[]{:S(2)}) collective-permute-start(bf16[64,512]{1,0:T(8,128)(2,1)S(1)} %get-tuple-element.54.refs_0_), channel_id=1, source_target_pairs={{0,198},{1,199},{2,196},{3,197},{4,194},{5,195},{6,192},{7,193},{8... | collective-permute-start | bytes 196616 | tf_op jit(solution)/shard_map/ppermute | solution.py:50
  73.5 1.6 %collective-permute-start.13 = (bf16[64,512]{1,0:T(8,128)(2,1)S(1)}, bf16[64,512]{1,0:T(8,128)(2,1)S(1)}, u32[]{:S(2)}, u32[]{:S(2)}) collective-permute-start(bf16[64,512]{1,0:T(8,128)(2,1)S(1)} %get-tuple-element.54.refs_0_), channel_id=1, source_target_pairs={{0,192},{1,193},{2,194},{3,195},{4,196},{5,197},{6,198},{7,199},{8... | collective-permute-start | bytes 196616 | tf_op jit(solution)/shard_map/ppermute | solution.py:50
  75.0 2.0 %collective-permute-start.12 = (bf16[64,512]{1,0:T(8,128)(2,1)S(1)}, bf16[64,512]{1,0:T(8,128)(2,1)S(1)}, u32[]{:S(2)}, u32[]{:S(2)}) collective-permute-start(bf16[64,512]{1,0:T(8,128)(2,1)S(1)} %get-tuple-element.54.refs_0_), channel_id=1, source_target_pairs={{0,6},{1,7},{2,4},{3,5},{4,2},{5,3},{6,0},{7,1},{8,10},{9,11},{10,... | collective-permute-start | bytes 196616 | tf_op jit(solution)/shard_map/ppermute | solution.py:50
  77.1 1.7 %collective-permute-done.14.refs_3_ = bf16[64,512]{1,0:T(8,128)(2,1)S(1)} collective-permute-done((bf16[64,512]{1,0:T(8,128)(2,1)S(1)}, bf16[64,512]{1,0:T(8,128)(2,1)S(1)}, u32[]{:S(2)}, u32[]{:S(2)}) %collective-permute-start.14) | collective-permute-done | bytes 65568 | tf_op jit(solution)/shard_map/ppermute | solution.py:50
  78.8 0.6 collective-permute-done.13.refs_2_
  79.4 1.1 %collective-permute-done.12.refs_1_ = bf16[64,512]{1,0:T(8,128)(2,1)S(1)} collective-permute-done((bf16[64,512]{1,0:T(8,128)(2,1)S(1)}, bf16[64,512]{1,0:T(8,128)(2,1)S(1)}, u32[]{:S(2)}, u32[]{:S(2)}) %collective-permute-start.12) | collective-permute-done | bytes 65568 | tf_op jit(solution)/shard_map/ppermute | solution.py:50
  80.5 0.1 collective-permute-start.17
  80.6 0.3 collective-permute-start.16
  80.9 3.2 %collective-permute-start.15 = (bf16[256,512]{1,0:T(8,128)(2,1)S(1)}, bf16[256,512]{1,0:T(8,128)(2,1)S(1)}, u32[]{:S(2)}, u32[]{:S(2)}) collective-permute-start(bf16[256,512]{1,0:T(8,128)(2,1)S(1)} %shard_map.190.own), channel_id=1, source_target_pairs={{0,2},{1,3},{2,0},{3,1},{4,6},{5,7},{6,4},{7,5},{8,14},{9,15},{10,... | collective-permute-start | bytes 786440 | tf_op jit(solution)/shard_map/ppermute | solution.py:50
  84.1 3.8 %collective-permute-start.18 = (bf16[2,96,512]{2,1,0:T(8,128)(2,1)S(1)}, bf16[2,96,512]{2,1,0:T(8,128)(2,1)S(1)}, u32[]{:S(2)}, u32[]{:S(2)}) collective-permute-start(bf16[2,96,512]{2,1,0:T(8,128)(2,1)S(1)} %get-tuple-element.56), channel_id=1, source_target_pairs={{1,0},{2,1},{3,2},{4,3},{5,4},{6,5},{7,6},{9,8},{10,9},{11,10},{12... | collective-permute-start | bytes 589832 | tf_op jit(solution)/shard_map/ppermute | solution.py:381
  87.9 2.0 %collective-permute-start.19 = (bf16[2,96,512]{2,1,0:T(8,128)(2,1)S(1)}, bf16[2,96,512]{2,1,0:T(8,128)(2,1)S(1)}, u32[]{:S(2)}, u32[]{:S(2)}) collective-permute-start(bf16[2,96,512]{2,1,0:T(8,128)(2,1)S(1)} %get-tuple-element.57), channel_id=1, source_target_pairs={{0,1},{1,2},{2,3},{3,4},{4,5},{5,6},{6,7},{8,9},{9,10},{10,11},{11... | collective-permute-start | bytes 589832 | tf_op jit(solution)/shard_map/ppermute | solution.py:381
  90.0 1.7 %collective-permute-done.18.cross_m = bf16[2,96,512]{2,1,0:T(8,128)(2,1)S(1)} collective-permute-done((bf16[2,96,512]{2,1,0:T(8,128)(2,1)S(1)}, bf16[2,96,512]{2,1,0:T(8,128)(2,1)S(1)}, u32[]{:S(2)}, u32[]{:S(2)}) %collective-permute-start.18) | collective-permute-done | bytes 196640 | tf_op jit(solution)/shard_map/ppermute | solution.py:381
  91.7 4.7 %collective-permute-done.19.cross_p = bf16[2,96,512]{2,1,0:T(8,128)(2,1)S(1)} collective-permute-done((bf16[2,96,512]{2,1,0:T(8,128)(2,1)S(1)}, bf16[2,96,512]{2,1,0:T(8,128)(2,1)S(1)}, u32[]{:S(2)}, u32[]{:S(2)}) %collective-permute-start.19) | collective-permute-done | bytes 196640 | tf_op jit(solution)/shard_map/ppermute | solution.py:381
  96.4 0.0 collective-permute-done.17.r3
  96.4 0.0 collective-permute-done.16.r2
  96.4 0.0 collective-permute-done.15.r1
  96.4 0.1 shard_map.191
  96.5 0.1 collective-permute-start.20
  96.6 0.9 shard_map.192
  97.5 1.8 %collective-permute-done.20.other = bf16[1040,512]{1,0:T(8,128)(2,1)S(1)} collective-permute-done((bf16[1040,512]{1,0:T(8,128)(2,1)S(1)}, bf16[1040,512]{1,0:T(8,128)(2,1)S(1)}, u32[]{:S(2)}, u32[]{:S(2)}) %collective-permute-start.20) | collective-permute-done | bytes 1064992 | tf_op jit(solution)/shard_map/ppermute | solution.py:50
  99.3 2.9 %shard_map.193 = (f32[2048,512]{1,0:T(8,128)}, f32[8,128]{1,0:T(8,128)}) custom-call(bf16[1040,512]{1,0:T(8,128)(2,1)S(1)} %get-tuple-element.58.own, bf16[1040,512]{1,0:T(8,128)(2,1)S(1)} %collective-permute-done.20.other, f32[8,512]{1,0:T(8,128)S(1)} %get-tuple-element.63.own_sq), custom_call_target="tpu_custom_call" | custom-call | tf_op jit(solution)/shard_map/pallas_call | solution.py:364
  (5 shorter events, 0.1 us)
Async XLA Ops:
  14.0 2.8 %collective-permute-start = (bf16[1040,512]{1,0:T(8,128)(2,1)S(1)}, bf16[1040,512]{1,0:T(8,128)(2,1)S(1)}, u32[]{:S(2)}, u32[]{:S(2)}) collective-permute-start(bf16[1040,512]{1,0:T(8,128)(2,1)S(1)} %get-tuple-element.37), channel_id=1, source_target_pairs={{0,8},{1,9},{2,10},{3,11},{4,12},{5,13},{6,14},{7,15},{8,0},{9,1},... | collective-permute-start | bytes 3194888 | tf_op jit(solution)/shard_map/ppermute | solution.py:50
  17.0 10.2 %collective-permute-start.1 = (bf16[272,512]{1,0:T(8,128)(2,1)S(1)}, bf16[272,512]{1,0:T(8,128)(2,1)S(1)}, u32[]{:S(2)}, u32[]{:S(2)}) collective-permute-start(bf16[272,512]{1,0:T(8,128)(2,1)S(1)} %get-tuple-element.42), channel_id=1, source_target_pairs={{0,2},{1,3},{2,0},{3,1},{4,6},{5,7},{6,4},{7,5},{8,14},{9,15},{10,... | collective-permute-start | bytes 835592 | tf_op jit(solution)/shard_map/ppermute | solution.py:50
  17.9 9.3 %collective-permute-start.2 = (bf16[272,512]{1,0:T(8,128)(2,1)S(1)}, bf16[272,512]{1,0:T(8,128)(2,1)S(1)}, u32[]{:S(2)}, u32[]{:S(2)}) collective-permute-start(bf16[272,512]{1,0:T(8,128)(2,1)S(1)} %get-tuple-element.43), channel_id=1, source_target_pairs={{0,64},{1,65},{2,66},{3,67},{4,68},{5,69},{6,70},{7,71},{8,200},{9... | collective-permute-start | bytes 835592 | tf_op jit(solution)/shard_map/ppermute | solution.py:50
  19.5 8.1 %collective-permute-start.3 = (bf16[272,512]{1,0:T(8,128)(2,1)S(1)}, bf16[272,512]{1,0:T(8,128)(2,1)S(1)}, u32[]{:S(2)}, u32[]{:S(2)}) collective-permute-start(bf16[272,512]{1,0:T(8,128)(2,1)S(1)} %get-tuple-element.44), channel_id=1, source_target_pairs={{0,66},{1,67},{2,64},{3,65},{4,70},{5,71},{6,68},{7,69},{8,206},{9... | collective-permute-start | bytes 835592 | tf_op jit(solution)/shard_map/ppermute | solution.py:50
  20.6 5.6 %collective-permute-start.4 = (bf16[2,96,512]{2,1,0:T(8,128)(2,1)S(1)}, bf16[2,96,512]{2,1,0:T(8,128)(2,1)S(1)}, u32[]{:S(2)}, u32[]{:S(2)}) collective-permute-start(bf16[2,96,512]{2,1,0:T(8,128)(2,1)S(1)} %get-tuple-element.45), channel_id=1, source_target_pairs={{8,0},{16,8},{24,16},{32,24},{40,32},{48,40},{56,48},{64,56},{72,6... | collective-permute-start | bytes 589832 | tf_op jit(solution)/shard_map/ppermute | solution.py:381
  21.9 5.4 %collective-permute-start.5 = (bf16[2,96,512]{2,1,0:T(8,128)(2,1)S(1)}, bf16[2,96,512]{2,1,0:T(8,128)(2,1)S(1)}, u32[]{:S(2)}, u32[]{:S(2)}) collective-permute-start(bf16[2,96,512]{2,1,0:T(8,128)(2,1)S(1)} %get-tuple-element.46), channel_id=1, source_target_pairs={{0,8},{8,16},{16,24},{24,32},{32,40},{40,48},{48,56},{56,64},{64,7... | collective-permute-start | bytes 589832 | tf_op jit(solution)/shard_map/ppermute | solution.py:381
  27.8 18.7 %collective-permute-start.6 = (bf16[80,512]{1,0:T(8,128)(2,1)S(1)}, bf16[80,512]{1,0:T(8,128)(2,1)S(1)}, u32[]{:S(2)}, u32[]{:S(2)}) collective-permute-start(bf16[80,512]{1,0:T(8,128)(2,1)S(1)} %get-tuple-element.51), channel_id=1, source_target_pairs={{0,6},{1,7},{2,4},{3,5},{4,2},{5,3},{6,0},{7,1},{8,10},{9,11},{10,... | collective-permute-start | bytes 245768 | tf_op jit(solution)/shard_map/ppermute | solution.py:50
  29.6 17.0 %collective-permute-start.7 = (bf16[80,512]{1,0:T(8,128)(2,1)S(1)}, bf16[80,512]{1,0:T(8,128)(2,1)S(1)}, u32[]{:S(2)}, u32[]{:S(2)}) collective-permute-start(bf16[80,512]{1,0:T(8,128)(2,1)S(1)} %get-tuple-element.52), channel_id=1, source_target_pairs={{0,192},{1,193},{2,194},{3,195},{4,196},{5,197},{6,198},{7,199},{8... | collective-permute-start | bytes 245768 | tf_op jit(solution)/shard_map/ppermute | solution.py:50
  44.2 7.8 %collective-permute-start.8 = (bf16[80,512]{1,0:T(8,128)(2,1)S(1)}, bf16[80,512]{1,0:T(8,128)(2,1)S(1)}, u32[]{:S(2)}, u32[]{:S(2)}) collective-permute-start(bf16[80,512]{1,0:T(8,128)(2,1)S(1)} %get-tuple-element.53), channel_id=1, source_target_pairs={{0,198},{1,199},{2,196},{3,197},{4,194},{5,195},{6,192},{7,193},{8... | collective-permute-start | bytes 245768 | tf_op jit(solution)/shard_map/ppermute | solution.py:50
  52.0 6.0 %collective-permute-start.9 = (f32[72,512]{1,0:T(8,128)S(1)}, f32[72,512]{1,0:T(8,128)S(1)}, u32[]{:S(2)}, u32[]{:S(2)}) collective-permute-start(f32[72,512]{1,0:T(8,128)S(1)} %shard_map.186.a), channel_id=1, source_target_pairs={{0,1},{1,0},{2,3},{3,2},{4,5},{5,4},{6,7},{7,6},{8,9},{9,8},{10,11... | collective-permute-start | bytes 442376 | tf_op jit(solution)/shard_map/ppermute | solution.py:50
  58.1 6.3 %collective-permute-start.10 = (bf16[80,512]{1,0:T(8,128)(2,1)S(1)}, bf16[80,512]{1,0:T(8,128)(2,1)S(1)}, u32[]{:S(2)}, u32[]{:S(2)}) collective-permute-start(bf16[80,512]{1,0:T(8,128)(2,1)S(1)} %shard_map.187.a), channel_id=1, source_target_pairs={{0,17},{1,16},{2,19},{3,18},{4,21},{5,20},{6,23},{7,22},{8,25},{9,... | collective-permute-start | bytes 245768 | tf_op jit(solution)/shard_map/ppermute | solution.py:50
  64.5 6.6 %collective-permute-start.11 = (bf16[80,512]{1,0:T(8,128)(2,1)S(1)}, bf16[80,512]{1,0:T(8,128)(2,1)S(1)}, u32[]{:S(2)}, u32[]{:S(2)}) collective-permute-start(bf16[80,512]{1,0:T(8,128)(2,1)S(1)} %shard_map.188.a), channel_id=1, source_target_pairs={{0,49},{1,48},{2,51},{3,50},{4,53},{5,52},{6,55},{7,54},{8,57},{9,... | collective-permute-start | bytes 245768 | tf_op jit(solution)/shard_map/ppermute | solution.py:50
  71.1 7.7 %collective-permute-start.14 = (bf16[64,512]{1,0:T(8,128)(2,1)S(1)}, bf16[64,512]{1,0:T(8,128)(2,1)S(1)}, u32[]{:S(2)}, u32[]{:S(2)}) collective-permute-start(bf16[64,512]{1,0:T(8,128)(2,1)S(1)} %get-tuple-element.54.refs_0_), channel_id=1, source_target_pairs={{0,198},{1,199},{2,196},{3,197},{4,194},{5,195},{6,192},{7,193},{8... | collective-permute-start | bytes 196616 | tf_op jit(solution)/shard_map/ppermute | solution.py:50
  73.5 6.0 %collective-permute-start.13 = (bf16[64,512]{1,0:T(8,128)(2,1)S(1)}, bf16[64,512]{1,0:T(8,128)(2,1)S(1)}, u32[]{:S(2)}, u32[]{:S(2)}) collective-permute-start(bf16[64,512]{1,0:T(8,128)(2,1)S(1)} %get-tuple-element.54.refs_0_), channel_id=1, source_target_pairs={{0,192},{1,193},{2,194},{3,195},{4,196},{5,197},{6,198},{7,199},{8... | collective-permute-start | bytes 196616 | tf_op jit(solution)/shard_map/ppermute | solution.py:50
  75.0 5.5 %collective-permute-start.12 = (bf16[64,512]{1,0:T(8,128)(2,1)S(1)}, bf16[64,512]{1,0:T(8,128)(2,1)S(1)}, u32[]{:S(2)}, u32[]{:S(2)}) collective-permute-start(bf16[64,512]{1,0:T(8,128)(2,1)S(1)} %get-tuple-element.54.refs_0_), channel_id=1, source_target_pairs={{0,6},{1,7},{2,4},{3,5},{4,2},{5,3},{6,0},{7,1},{8,10},{9,11},{10,... | collective-permute-start | bytes 196616 | tf_op jit(solution)/shard_map/ppermute | solution.py:50
  80.5 15.9 %collective-permute-start.17 = (bf16[256,512]{1,0:T(8,128)(2,1)S(1)}, bf16[256,512]{1,0:T(8,128)(2,1)S(1)}, u32[]{:S(2)}, u32[]{:S(2)}) collective-permute-start(bf16[256,512]{1,0:T(8,128)(2,1)S(1)} %shard_map.190.own), channel_id=1, source_target_pairs={{0,66},{1,67},{2,64},{3,65},{4,70},{5,71},{6,68},{7,69},{8,206},{9... | collective-permute-start | bytes 786440 | tf_op jit(solution)/shard_map/ppermute | solution.py:50
  80.6 15.8 %collective-permute-start.16 = (bf16[256,512]{1,0:T(8,128)(2,1)S(1)}, bf16[256,512]{1,0:T(8,128)(2,1)S(1)}, u32[]{:S(2)}, u32[]{:S(2)}) collective-permute-start(bf16[256,512]{1,0:T(8,128)(2,1)S(1)} %shard_map.190.own), channel_id=1, source_target_pairs={{0,64},{1,65},{2,66},{3,67},{4,68},{5,69},{6,70},{7,71},{8,200},{9... | collective-permute-start | bytes 786440 | tf_op jit(solution)/shard_map/ppermute | solution.py:50
  80.9 15.5 %collective-permute-start.15 = (bf16[256,512]{1,0:T(8,128)(2,1)S(1)}, bf16[256,512]{1,0:T(8,128)(2,1)S(1)}, u32[]{:S(2)}, u32[]{:S(2)}) collective-permute-start(bf16[256,512]{1,0:T(8,128)(2,1)S(1)} %shard_map.190.own), channel_id=1, source_target_pairs={{0,2},{1,3},{2,0},{3,1},{4,6},{5,7},{6,4},{7,5},{8,14},{9,15},{10,... | collective-permute-start | bytes 786440 | tf_op jit(solution)/shard_map/ppermute | solution.py:50
  84.1 7.6 %collective-permute-start.18 = (bf16[2,96,512]{2,1,0:T(8,128)(2,1)S(1)}, bf16[2,96,512]{2,1,0:T(8,128)(2,1)S(1)}, u32[]{:S(2)}, u32[]{:S(2)}) collective-permute-start(bf16[2,96,512]{2,1,0:T(8,128)(2,1)S(1)} %get-tuple-element.56), channel_id=1, source_target_pairs={{1,0},{2,1},{3,2},{4,3},{5,4},{6,5},{7,6},{9,8},{10,9},{11,10},{12... | collective-permute-start | bytes 589832 | tf_op jit(solution)/shard_map/ppermute | solution.py:381
  87.9 8.5 %collective-permute-start.19 = (bf16[2,96,512]{2,1,0:T(8,128)(2,1)S(1)}, bf16[2,96,512]{2,1,0:T(8,128)(2,1)S(1)}, u32[]{:S(2)}, u32[]{:S(2)}) collective-permute-start(bf16[2,96,512]{2,1,0:T(8,128)(2,1)S(1)} %get-tuple-element.57), channel_id=1, source_target_pairs={{0,1},{1,2},{2,3},{3,4},{4,5},{5,6},{6,7},{8,9},{9,10},{10,11},{11... | collective-permute-start | bytes 589832 | tf_op jit(solution)/shard_map/ppermute | solution.py:381
  96.5 2.8 %collective-permute-start.20 = (bf16[1040,512]{1,0:T(8,128)(2,1)S(1)}, bf16[1040,512]{1,0:T(8,128)(2,1)S(1)}, u32[]{:S(2)}, u32[]{:S(2)}) collective-permute-start(bf16[1040,512]{1,0:T(8,128)(2,1)S(1)} %get-tuple-element.58.own), channel_id=1, source_target_pairs={{0,8},{1,9},{2,10},{3,11},{4,12},{5,13},{6,14},{7,15},{8,0},{9,1},... | collective-permute-start | bytes 3194888 | tf_op jit(solution)/shard_map/ppermute | solution.py:50

commit v3 on v2

--- a/solution.py
+++ b/solution.py
@@ -4,6 +4,7 @@
 from jax.experimental import pallas as pl
 from jax.experimental.pallas import tpu as pltpu
 from jax.sharding import PartitionSpec as P
+
 
 F32 = jnp.float32
 BF16 = jnp.bfloat16
@@ -36,7 +37,7 @@
         if kind == "core":
             core ^= 1
         elif kind == "z":
-            label = (z ^ (z >> 1)) ^ flip
+            label = (z ^ (z >> 1)) ^ (1, 2, 4)[(flip + core) % 3]
             z = label ^ (label >> 1) ^ (label >> 2)
         else:
             bit = core if kind == "first" else 1 - core
@@ -224,15 +225,31 @@
     gate_out[...] = kept
 
 
-def after_core(own, gate, got, lead_m, lead_p, keep, gate_out, s1, s2, s3, o_lm, o_lp):
+def put_valid(dst, src, valid):
+    @pl.when(valid)
+    def _():
+        dst[...] = src[...]
+
+    @pl.when(jnp.logical_not(valid))
+    def _():
+        dst[...] = jnp.zeros(dst.shape, dst.dtype)
+
+
+def has_after(axis):
+    return lax.axis_index(axis) < lax.axis_size(axis) - 1
+
+
+def has_before(axis):
+    return lax.axis_index(axis) > 0
+
+
+def after_core(own, gate, got, keep, gate_out, s1, s2, s3):
     rows = own.shape[0]
     split_four(
         lambda lo, hi: own[lo:hi] + got[lo:hi].astype(F32),
         gate[...] + get_gate(got, rows),
         rows, keep, gate_out, (s1, s2, s3),
     )
-    o_lm[...] = lead_m[...]
-    o_lp[...] = lead_p[...]
 
 
 def four(own, got):
@@ -259,8 +276,9 @@
     for k in range(2):
         for ref, mid, cut in ((cross_m, mid_m, 0), (cross_p, mid_p, 2)):
             ref[k, 0:b] = mid[k]
-            ref[k, b : 2 * b] = lead_m[k, cut * b : (cut + 1) * b]
-            ref[k, 2 * b : 3 * b] = lead_p[k, cut * b : (cut + 1) * b]
+            rows = pl.ds(cut * b, b)
+            put_valid(ref.at[k, pl.ds(b, b)], lead_m.at[k, rows], has_after("tx"))
+            put_valid(ref.at[k, pl.ds(2 * b, b)], lead_p.at[k, rows], has_before("tx"))
 
 
 def after_second(own, gate, r1, r2, r3, out):
@@ -293,12 +311,6 @@
     for ref in refs[:-1]:
         out[row : row + ref.shape[0]] = ref[...]
         row += ref.shape[0]
-
-
-def join_through(own, r1, r2, r3, gate, cross_m, cross_p, out, o_cross_m, o_cross_p):
-    join(own, r1, r2, r3, gate, out)
-    o_cross_m[...] = cross_m[...]
-    o_cross_p[...] = cross_p[...]
 
 
 def squares(ref, label):
@@ -317,13 +329,15 @@
     _, mine, _ = my_labels()
     o_squares[...] = squares(own, mine)
     b = o_fresh.shape[0] // 8
+    l_m, l_p = (lead_m, has_after("tx")), (lead_p, has_before("tx"))
+    c_m, c_p = (cross_m, has_after("ty")), (cross_p, has_before("ty"))
     arrived = (
-        (cross_m, 1), (lead_m, 1), (cross_p, 1), (cross_m, 0),
-        (cross_p, 0), (cross_m, 2), (lead_p, 1), (cross_p, 2),
-    )
-    for d, (ref, cut) in enumerate(arrived):
-        o_fresh[d * b : (d + 1) * b] = ref[0, cut * b : (cut + 1) * b]
-        o_returned[(7 - d) * b : (8 - d) * b] = ref[1, cut * b : (cut + 1) * b]
+        (c_m, 1), (l_m, 1), (c_p, 1), (c_m, 0), (c_p, 0), (c_m, 2), (l_p, 1), (c_p, 2),
+    )
+    for d, ((ref, valid), cut) in enumerate(arrived):
+        rows = pl.ds(cut * b, b)
+        put_valid(o_fresh.at[pl.ds(d * b, b)], ref.at[0, rows], valid)
+        put_valid(o_returned.at[pl.ds((7 - d) * b, b)], ref.at[1, rows], valid)
 
 
 def last_kernel(own, other, own_sq, o_layers, o_gate, whole, sems):
@@ -375,10 +389,9 @@
     return jax.ShapeDtypeStruct((rows, w), kind)
 
 
-def from_behind(value, axis, steps):
+def shift(value, axis, steps):
     count = lax.axis_size(axis)
-    first, last = (max(0, -steps), min(count, count - steps))
-    return lax.ppermute(value, axis, [(source, source + steps) for source in range(first, last)])
+    return lax.ppermute(value, axis, [(k, (k + steps) % count) for k in range(count)])
 
 
 def on_device(
@@ -462,32 +475,28 @@
 
     wide = jax.ShapeDtypeStruct((2, 3 * b, w), BF16)
     got = swap(send, "core")
+    lead_m = shift(lead_m, "tx", -1)
+    lead_p = shift(lead_p, "tx", 1)
     part = n // 2
-    keep, gate, s1, s2, s3, lead_m, lead_p = call(
-        after_core, quarter(part) + (wide, wide), keep, gate, got, lead_m, lead_p
-    )
-    got = [swap(value, "first", j) for j, value in ((1, s1), (2, s2), (3, s3))]
-    lead_m = from_behind(lead_m, "tx", -1)
-    lead_p = from_behind(lead_p, "tx", 1)
+    keep, gate, s1, s2, s3 = call(after_core, quarter(part), keep, gate, got)
+    sends = ((1, s1), (2, s2), (3, s3))
+    got = [swap(value, "first", j) for j, value in sends]
     part = part // 4
     keep, gate, s1, s2, s3, cross_m, cross_p = call(
         after_first, quarter(part) + (wide, wide), keep, gate, *got, lead_m, lead_p, mid_m, mid_p
     )
-    got = [swap(value, "second", j) for j, value in ((1, s1), (2, s2), (3, s3))]
+    sends = ((1, s1), (2, s2), (3, s3))
+    got = [swap(value, "second", j) for j, value in sends]
+    cross_m = shift(cross_m, "ty", -1)
     (both,) = call(after_second, (shape(part + 8, w, F32),), keep, gate, *got)
-    (both,) = call(add_wide, (shape(part + 16, w, BF16),), both, swap(both, "z", 1))
-    (both,) = call(add_narrow, (shape(part + 16, w, BF16),), both, swap(both, "z", 2))
-    own, gate = call(
-        add_last, (shape(part, w, BF16), shape(16, w, BF16)), both, swap(both, "z", 4)
-    )
+    (both,) = call(add_wide, (shape(part + 16, w, BF16),), both, swap(both, "z", 0))
+    (both,) = call(add_narrow, (shape(part + 16, w, BF16),), both, swap(both, "z", 1))
+    own, gate = call(add_last, (shape(part, w, BF16), shape(16, w, BF16)), both, swap(both, "z", 2))
     got = [swap(own, "second", j) for j in (1, 2, 3)]
+    cross_p = shift(cross_p, "ty", 1)
     (own,) = call(join, (shape(4 * part, w, BF16),), own, *got)
     got = [swap(own, "first", j) for j in (1, 2, 3)]
-    cross_m = from_behind(cross_m, "ty", -1)
-    cross_p = from_behind(cross_p, "ty", 1)
-    own, cross_m, cross_p = call(
-        join_through, (shape(16 * part + 16, w, BF16), wide, wide), own, *got, gate, cross_m, cross_p
-    )
+    (own,) = call(join, (shape(16 * part + 16, w, BF16),), own, *got, gate)
     other = swap(own, "core")
     own_sq, fresh, returned = call(
         own_squares, (shape(8, w, F32), shape(h, w, BF16), shape(h, w, BF16)),

time: 103 us -> 107 us (1.039)
  the two profiles are of different devices: /device:TPU:6 before, /device:TPU:17 now
where the time goes in v3:
time: 107 us
  starting transfers between devices  51.3 us (48%)
  waiting for transfers between devices  37.3 us (35%)
  Pallas kernels  17.2 us (16%)
  between operations  1.51 us (1%)
    ppermute x17, starting transfers between devices, swap(): return lax.ppermute(value, AXES, xor_pairs(kind, flip))  45.1 us
    ppermute x17, waiting for transfers between devices, swap(): return lax.ppermute(value, AXES, xor_pairs(kind, flip))  22.5 us
    ppermute x4, waiting for transfers between devices, shift(): lax.ppermute(value, axis, [(k, (k + steps) % count) for k in range(count)])  14.9 us
    pallas_call x1, Pallas kernels, on_device(): pl.pallas_call(tile_kernel, out_shape=outs, in_specs=[pl.BlockSpec(memory...  12.8 us
    ppermute x4, starting transfers between devices, shift(): lax.ppermute(value, axis, [(k, (k + steps) % count) for k in range(count)])  6.25 us
    pallas_call x10, Pallas kernels, call(): pl.pallas_call(kernel, out_shape=outs, in_specs=[vmem] * len(args), out_s...  4.4 us
  transfers between devices with their start and end apart: 21, of which 16 were waited for; matrix products, arithmetic and copies ran while one was open for 0% of the time, Pallas kernels for 1%

profile of v3, /device:TPU:17, one launch (start us, length us, event | category | flops | bytes accessed | tf_op | source)
XLA Modules:
  0.0 107.3 jit_solution(11402775316441224383)
XLA Ops:
  1.3 12.8 %shard_map.183 = (bf16[2,96,512]{2,1,0:T(8,128)(2,1)S(1)}, bf16[2,96,512]{2,1,0:T(8,128)(2,1)S(1)}, bf16[2,32,512]{2,1,0:T(8,128)(2,1)S(1)}, bf16[2,32,512]{2,1,...) custom-call(s32[1,1]{1,0:T(1,128)S(6)} %copy.20.live_ref, ...), custom_call_target="tpu_custom_call" | custom-call | tf_op jit(solution)/shard_map/pallas_call | solution.py:420
  14.1 0.8 collective-permute-start
  14.8 2.3 %collective-permute-done.got = bf16[1040,512]{1,0:T(8,128)(2,1)S(1)} collective-permute-done((bf16[1040,512]{1,0:T(8,128)(2,1)S(1)}, bf16[1040,512]{1,0:T(8,128)(2,1)S(1)}, u32[]{:S(2)}, u32[]{:S(2)}) %collective-permute-start) | collective-permute-done | bytes 1064992 | tf_op jit(solution)/shard_map/ppermute | solution.py:51
  17.1 0.2 shard_map.184
  17.3 2.6 %collective-permute-start.1 = (bf16[272,512]{1,0:T(8,128)(2,1)S(1)}, bf16[272,512]{1,0:T(8,128)(2,1)S(1)}, u32[]{:S(2)}, u32[]{:S(2)}) collective-permute-start(bf16[272,512]{1,0:T(8,128)(2,1)S(1)} %get-tuple-element.35), channel_id=1, source_target_pairs={{0,2},{1,3},{2,0},{3,1},{4,6},{5,7},{6,4},{7,5},{8,14},{9,15},{10,... | collective-permute-start | bytes 835592 | tf_op jit(solution)/shard_map/ppermute | solution.py:51
  19.9 0.2 collective-permute-start.2
  20.0 1.2 %collective-permute-start.3 = (bf16[272,512]{1,0:T(8,128)(2,1)S(1)}, bf16[272,512]{1,0:T(8,128)(2,1)S(1)}, u32[]{:S(2)}, u32[]{:S(2)}) collective-permute-start(bf16[272,512]{1,0:T(8,128)(2,1)S(1)} %get-tuple-element.37), channel_id=1, source_target_pairs={{0,66},{1,67},{2,64},{3,65},{4,70},{5,71},{6,68},{7,69},{8,206},{9... | collective-permute-start | bytes 835592 | tf_op jit(solution)/shard_map/ppermute | solution.py:51
  21.2 0.0 collective-permute-start.4
  21.3 2.9 %collective-permute-start.5 = (bf16[2,96,512]{2,1,0:T(8,128)(2,1)S(1)}, bf16[2,96,512]{2,1,0:T(8,128)(2,1)S(1)}, u32[]{:S(2)}, u32[]{:S(2)}) collective-permute-start(bf16[2,96,512]{2,1,0:T(8,128)(2,1)S(1)} %get-tuple-element.39), channel_id=1, source_target_pairs={{0,8},{8,16},{16,24},{24,32},{32,40},{40,48},{48,56},{56,64},{64,7... | collective-permute-start | bytes 589832 | tf_op jit(solution)/shard_map/ppermute | solution.py:394
  24.1 5.5 %collective-permute-done.4.lead_m = bf16[2,96,512]{2,1,0:T(8,128)(2,1)S(1)} collective-permute-done((bf16[2,96,512]{2,1,0:T(8,128)(2,1)S(1)}, bf16[2,96,512]{2,1,0:T(8,128)(2,1)S(1)}, u32[]{:S(2)}, u32[]{:S(2)}) %collective-permute-start.4) | collective-permute-done | bytes 196640 | tf_op jit(solution)/shard_map/ppermute | solution.py:394
  29.6 0.0 collective-permute-done.5.lead_p
  29.6 0.0 collective-permute-done.1.r1
  29.6 0.0 collective-permute-done.2.r2
  29.6 0.0 collective-permute-done.3.r3
  29.6 0.2 shard_map.185
  29.8 1.4 %collective-permute-start.6 = (bf16[80,512]{1,0:T(8,128)(2,1)S(1)}, bf16[80,512]{1,0:T(8,128)(2,1)S(1)}, u32[]{:S(2)}, u32[]{:S(2)}) collective-permute-start(bf16[80,512]{1,0:T(8,128)(2,1)S(1)} %get-tuple-element.44), channel_id=1, source_target_pairs={{0,6},{1,7},{2,4},{3,5},{4,2},{5,3},{6,0},{7,1},{8,10},{9,11},{10,... | collective-permute-start | bytes 245768 | tf_op jit(solution)/shard_map/ppermute | solution.py:51
  31.2 1.0 collective-permute-start.7
  32.2 0.9 collective-permute-start.8
  33.2 0.3 collective-permute-done.6.r1
  33.5 1.3 %collective-permute-done.7.r2 = bf16[80,512]{1,0:T(8,128)(2,1)S(1)} collective-permute-done((bf16[80,512]{1,0:T(8,128)(2,1)S(1)}, bf16[80,512]{1,0:T(8,128)(2,1)S(1)}, u32[]{:S(2)}, u32[]{:S(2)}) %collective-permute-start.7) | collective-permute-done | bytes 81952 | tf_op jit(solution)/shard_map/ppermute | solution.py:51
  34.8 1.8 %collective-permute-done.8.r3 = bf16[80,512]{1,0:T(8,128)(2,1)S(1)} collective-permute-done((bf16[80,512]{1,0:T(8,128)(2,1)S(1)}, bf16[80,512]{1,0:T(8,128)(2,1)S(1)}, u32[]{:S(2)}, u32[]{:S(2)}) %collective-permute-start.8) | collective-permute-done | bytes 81952 | tf_op jit(solution)/shard_map/ppermute | solution.py:51
  36.7 4.2 %collective-permute-start.9 = (f32[72,512]{1,0:T(8,128)S(1)}, f32[72,512]{1,0:T(8,128)S(1)}, u32[]{:S(2)}, u32[]{:S(2)}) collective-permute-start(f32[72,512]{1,0:T(8,128)S(1)} %shard_map.186.a), channel_id=1, source_target_pairs={{0,1},{1,0},{2,3},{3,2},{4,5},{5,4},{6,7},{7,6},{8,25},{9,24},{10,... | collective-permute-start | bytes 442376 | tf_op jit(solution)/shard_map/ppermute | solution.py:51
  40.9 2.6 %collective-permute-done.9.b = f32[72,512]{1,0:T(8,128)S(1)} collective-permute-done((f32[72,512]{1,0:T(8,128)S(1)}, f32[72,512]{1,0:T(8,128)S(1)}, u32[]{:S(2)}, u32[]{:S(2)}) %collective-permute-start.9) | collective-permute-done | bytes 147488 | tf_op jit(solution)/shard_map/ppermute | solution.py:51
  43.6 7.2 %collective-permute-start.10 = (bf16[80,512]{1,0:T(8,128)(2,1)S(1)}, bf16[80,512]{1,0:T(8,128)(2,1)S(1)}, u32[]{:S(2)}, u32[]{:S(2)}) collective-permute-start(bf16[80,512]{1,0:T(8,128)(2,1)S(1)} %shard_map.187.a), channel_id=1, source_target_pairs={{0,17},{1,16},{2,19},{3,18},{4,21},{5,20},{6,23},{7,22},{8,57},{9,... | collective-permute-start | bytes 245768 | tf_op jit(solution)/shard_map/ppermute | solution.py:51
  50.7 1.8 %collective-permute-done.10.b = bf16[80,512]{1,0:T(8,128)(2,1)S(1)} collective-permute-done((bf16[80,512]{1,0:T(8,128)(2,1)S(1)}, bf16[80,512]{1,0:T(8,128)(2,1)S(1)}, u32[]{:S(2)}, u32[]{:S(2)}) %collective-permute-start.10) | collective-permute-done | bytes 81952 | tf_op jit(solution)/shard_map/ppermute | solution.py:51
  52.6 2.5 %collective-permute-start.11 = (bf16[80,512]{1,0:T(8,128)(2,1)S(1)}, bf16[80,512]{1,0:T(8,128)(2,1)S(1)}, u32[]{:S(2)}, u32[]{:S(2)}) collective-permute-start(bf16[80,512]{1,0:T(8,128)(2,1)S(1)} %shard_map.188.a), channel_id=1, source_target_pairs={{0,49},{1,48},{2,51},{3,50},{4,53},{5,52},{6,55},{7,54},{8,9},{9,8... | collective-permute-start | bytes 245768 | tf_op jit(solution)/shard_map/ppermute | solution.py:51
  55.1 2.0 %collective-permute-done.11.b = bf16[80,512]{1,0:T(8,128)(2,1)S(1)} collective-permute-done((bf16[80,512]{1,0:T(8,128)(2,1)S(1)}, bf16[80,512]{1,0:T(8,128)(2,1)S(1)}, u32[]{:S(2)}, u32[]{:S(2)}) %collective-permute-start.11) | collective-permute-done | bytes 81952 | tf_op jit(solution)/shard_map/ppermute | solution.py:51
  57.1 1.4 %collective-permute-start.14 = (bf16[64,512]{1,0:T(8,128)(2,1)S(1)}, bf16[64,512]{1,0:T(8,128)(2,1)S(1)}, u32[]{:S(2)}, u32[]{:S(2)}) collective-permute-start(bf16[64,512]{1,0:T(8,128)(2,1)S(1)} %get-tuple-element.47.refs_0_), channel_id=1, source_target_pairs={{0,198},{1,199},{2,196},{3,197},{4,194},{5,195},{6,192},{7,193},{8... | collective-permute-start | bytes 196616 | tf_op jit(solution)/shard_map/ppermute | solution.py:51
  58.6 1.2 %collective-permute-start.13 = (bf16[64,512]{1,0:T(8,128)(2,1)S(1)}, bf16[64,512]{1,0:T(8,128)(2,1)S(1)}, u32[]{:S(2)}, u32[]{:S(2)}) collective-permute-start(bf16[64,512]{1,0:T(8,128)(2,1)S(1)} %get-tuple-element.47.refs_0_), channel_id=1, source_target_pairs={{0,192},{1,193},{2,194},{3,195},{4,196},{5,197},{6,198},{7,199},{8... | collective-permute-start | bytes 196616 | tf_op jit(solution)/shard_map/ppermute | solution.py:51
  59.8 0.1 collective-permute-start.12
  59.9 1.4 %collective-permute-done.14.refs_3_ = bf16[64,512]{1,0:T(8,128)(2,1)S(1)} collective-permute-done((bf16[64,512]{1,0:T(8,128)(2,1)S(1)}, bf16[64,512]{1,0:T(8,128)(2,1)S(1)}, u32[]{:S(2)}, u32[]{:S(2)}) %collective-permute-start.14) | collective-permute-done | bytes 65568 | tf_op jit(solution)/shard_map/ppermute | solution.py:51
  61.3 0.7 collective-permute-done.13.refs_2_
  61.9 1.0 collective-permute-done.12.refs_1_
  62.9 0.7 collective-permute-start.17
  63.6 4.6 %collective-permute-start.16 = (bf16[256,512]{1,0:T(8,128)(2,1)S(1)}, bf16[256,512]{1,0:T(8,128)(2,1)S(1)}, u32[]{:S(2)}, u32[]{:S(2)}) collective-permute-start(bf16[256,512]{1,0:T(8,128)(2,1)S(1)} %shard_map.190.refs_0_), channel_id=1, source_target_pairs={{0,64},{1,65},{2,66},{3,67},{4,68},{5,69},{6,70},{7,71},{8,200},{9... | collective-permute-start | bytes 786440 | tf_op jit(solution)/shard_map/ppermute | solution.py:51
  68.2 0.0 collective-permute-start.15
  68.2 2.3 %collective-permute-done.17.refs_3_ = bf16[256,512]{1,0:T(8,128)(2,1)S(1)} collective-permute-done((bf16[256,512]{1,0:T(8,128)(2,1)S(1)}, bf16[256,512]{1,0:T(8,128)(2,1)S(1)}, u32[]{:S(2)}, u32[]{:S(2)}) %collective-permute-start.17) | collective-permute-done | bytes 262176 | tf_op jit(solution)/shard_map/ppermute | solution.py:51
  70.5 4.4 %collective-permute-done.16.refs_2_ = bf16[256,512]{1,0:T(8,128)(2,1)S(1)} collective-permute-done((bf16[256,512]{1,0:T(8,128)(2,1)S(1)}, bf16[256,512]{1,0:T(8,128)(2,1)S(1)}, u32[]{:S(2)}, u32[]{:S(2)}) %collective-permute-start.16) | collective-permute-done | bytes 262176 | tf_op jit(solution)/shard_map/ppermute | solution.py:51
  74.9 0.5 collective-permute-done.15.refs_1_
  75.4 0.1 shard_map.191.own
  75.4 15.1 %collective-permute-start.20 = (bf16[1040,512]{1,0:T(8,128)(2,1)S(1)}, bf16[1040,512]{1,0:T(8,128)(2,1)S(1)}, u32[]{:S(2)}, u32[]{:S(2)}) collective-permute-start(bf16[1040,512]{1,0:T(8,128)(2,1)S(1)} %shard_map.191.own), channel_id=1, source_target_pairs={{0,8},{1,9},{2,10},{3,11},{4,12},{5,13},{6,14},{7,15},{8,0},{9,1},... | collective-permute-start | bytes 3194888 | tf_op jit(solution)/shard_map/ppermute | solution.py:51
  90.6 3.4 %collective-permute-start.18 = (bf16[2,96,512]{2,1,0:T(8,128)(2,1)S(1)}, bf16[2,96,512]{2,1,0:T(8,128)(2,1)S(1)}, u32[]{:S(2)}, u32[]{:S(2)}) collective-permute-start(bf16[2,96,512]{2,1,0:T(8,128)(2,1)S(1)} %get-tuple-element.49), channel_id=1, source_target_pairs={{0,7},{1,0},{2,1},{3,2},{4,3},{5,4},{6,5},{7,6},{8,15},{9,8},{10,9... | collective-permute-start | bytes 589832 | tf_op jit(solution)/shard_map/ppermute | solution.py:394
  93.9 0.0 collective-permute-start.19
  93.9 4.2 %collective-permute-done.18.cross_m = bf16[2,96,512]{2,1,0:T(8,128)(2,1)S(1)} collective-permute-done((bf16[2,96,512]{2,1,0:T(8,128)(2,1)S(1)}, bf16[2,96,512]{2,1,0:T(8,128)(2,1)S(1)}, u32[]{:S(2)}, u32[]{:S(2)}) %collective-permute-start.18) | collective-permute-done | bytes 196640 | tf_op jit(solution)/shard_map/ppermute | solution.py:394
  98.1 5.2 %collective-permute-done.19.cross_p = bf16[2,96,512]{2,1,0:T(8,128)(2,1)S(1)} collective-permute-done((bf16[2,96,512]{2,1,0:T(8,128)(2,1)S(1)}, bf16[2,96,512]{2,1,0:T(8,128)(2,1)S(1)}, u32[]{:S(2)}, u32[]{:S(2)}) %collective-permute-start.19) | collective-permute-done | bytes 196640 | tf_op jit(solution)/shard_map/ppermute | solution.py:394
  103.3 1.0 shard_map.192
  104.3 0.0 collective-permute-done.20.other
  104.3 2.9 %shard_map.193 = (f32[2048,512]{1,0:T(8,128)}, f32[8,128]{1,0:T(8,128)}) custom-call(bf16[1040,512]{1,0:T(8,128)(2,1)S(1)} %shard_map.191.own, bf16[1040,512]{1,0:T(8,128)(2,1)S(1)} %collective-permute-done.20.other, f32[8,512]{1,0:T(8,128)S(1)} %get-tuple-element.53.own_sq), custom_call_target="tpu_custom_call" | custom-call | tf_op jit(solution)/shard_map/pallas_call | solution.py:378
  (5 shorter events, 0.1 us)
Async XLA Ops:
  14.1 3.1 %collective-permute-start = (bf16[1040,512]{1,0:T(8,128)(2,1)S(1)}, bf16[1040,512]{1,0:T(8,128)(2,1)S(1)}, u32[]{:S(2)}, u32[]{:S(2)}) collective-permute-start(bf16[1040,512]{1,0:T(8,128)(2,1)S(1)} %get-tuple-element.32), channel_id=1, source_target_pairs={{0,8},{1,9},{2,10},{3,11},{4,12},{5,13},{6,14},{7,15},{8,0},{9,1},... | collective-permute-start | bytes 3194888 | tf_op jit(solution)/shard_map/ppermute | solution.py:51
  17.3 12.3 %collective-permute-start.1 = (bf16[272,512]{1,0:T(8,128)(2,1)S(1)}, bf16[272,512]{1,0:T(8,128)(2,1)S(1)}, u32[]{:S(2)}, u32[]{:S(2)}) collective-permute-start(bf16[272,512]{1,0:T(8,128)(2,1)S(1)} %get-tuple-element.35), channel_id=1, source_target_pairs={{0,2},{1,3},{2,0},{3,1},{4,6},{5,7},{6,4},{7,5},{8,14},{9,15},{10,... | collective-permute-start | bytes 835592 | tf_op jit(solution)/shard_map/ppermute | solution.py:51
  19.9 9.7 %collective-permute-start.2 = (bf16[272,512]{1,0:T(8,128)(2,1)S(1)}, bf16[272,512]{1,0:T(8,128)(2,1)S(1)}, u32[]{:S(2)}, u32[]{:S(2)}) collective-permute-start(bf16[272,512]{1,0:T(8,128)(2,1)S(1)} %get-tuple-element.36), channel_id=1, source_target_pairs={{0,64},{1,65},{2,66},{3,67},{4,68},{5,69},{6,70},{7,71},{8,200},{9... | collective-permute-start | bytes 835592 | tf_op jit(solution)/shard_map/ppermute | solution.py:51
  20.0 9.6 %collective-permute-start.3 = (bf16[272,512]{1,0:T(8,128)(2,1)S(1)}, bf16[272,512]{1,0:T(8,128)(2,1)S(1)}, u32[]{:S(2)}, u32[]{:S(2)}) collective-permute-start(bf16[272,512]{1,0:T(8,128)(2,1)S(1)} %get-tuple-element.37), channel_id=1, source_target_pairs={{0,66},{1,67},{2,64},{3,65},{4,70},{5,71},{6,68},{7,69},{8,206},{9... | collective-permute-start | bytes 835592 | tf_op jit(solution)/shard_map/ppermute | solution.py:51
  21.2 8.4 %collective-permute-start.4 = (bf16[2,96,512]{2,1,0:T(8,128)(2,1)S(1)}, bf16[2,96,512]{2,1,0:T(8,128)(2,1)S(1)}, u32[]{:S(2)}, u32[]{:S(2)}) collective-permute-start(bf16[2,96,512]{2,1,0:T(8,128)(2,1)S(1)} %get-tuple-element.38), channel_id=1, source_target_pairs={{0,248},{8,0},{16,8},{24,16},{32,24},{40,32},{48,40},{56,48},{64,5... | collective-permute-start | bytes 589832 | tf_op jit(solution)/shard_map/ppermute | solution.py:394
  21.3 8.4 %collective-permute-start.5 = (bf16[2,96,512]{2,1,0:T(8,128)(2,1)S(1)}, bf16[2,96,512]{2,1,0:T(8,128)(2,1)S(1)}, u32[]{:S(2)}, u32[]{:S(2)}) collective-permute-start(bf16[2,96,512]{2,1,0:T(8,128)(2,1)S(1)} %get-tuple-element.39), channel_id=1, source_target_pairs={{0,8},{8,16},{16,24},{24,32},{32,40},{40,48},{48,56},{56,64},{64,7... | collective-permute-start | bytes 589832 | tf_op jit(solution)/shard_map/ppermute | solution.py:394
  29.8 3.7 %collective-permute-start.6 = (bf16[80,512]{1,0:T(8,128)(2,1)S(1)}, bf16[80,512]{1,0:T(8,128)(2,1)S(1)}, u32[]{:S(2)}, u32[]{:S(2)}) collective-permute-start(bf16[80,512]{1,0:T(8,128)(2,1)S(1)} %get-tuple-element.44), channel_id=1, source_target_pairs={{0,6},{1,7},{2,4},{3,5},{4,2},{5,3},{6,0},{7,1},{8,10},{9,11},{10,... | collective-permute-start | bytes 245768 | tf_op jit(solution)/shard_map/ppermute | solution.py:51
  31.2 3.6 %collective-permute-start.7 = (bf16[80,512]{1,0:T(8,128)(2,1)S(1)}, bf16[80,512]{1,0:T(8,128)(2,1)S(1)}, u32[]{:S(2)}, u32[]{:S(2)}) collective-permute-start(bf16[80,512]{1,0:T(8,128)(2,1)S(1)} %get-tuple-element.45), channel_id=1, source_target_pairs={{0,192},{1,193},{2,194},{3,195},{4,196},{5,197},{6,198},{7,199},{8... | collective-permute-start | bytes 245768 | tf_op jit(solution)/shard_map/ppermute | solution.py:51
  32.2 4.4 %collective-permute-start.8 = (bf16[80,512]{1,0:T(8,128)(2,1)S(1)}, bf16[80,512]{1,0:T(8,128)(2,1)S(1)}, u32[]{:S(2)}, u32[]{:S(2)}) collective-permute-start(bf16[80,512]{1,0:T(8,128)(2,1)S(1)} %get-tuple-element.46), channel_id=1, source_target_pairs={{0,198},{1,199},{2,196},{3,197},{4,194},{5,195},{6,192},{7,193},{8... | collective-permute-start | bytes 245768 | tf_op jit(solution)/shard_map/ppermute | solution.py:51
  36.7 6.9 %collective-permute-start.9 = (f32[72,512]{1,0:T(8,128)S(1)}, f32[72,512]{1,0:T(8,128)S(1)}, u32[]{:S(2)}, u32[]{:S(2)}) collective-permute-start(f32[72,512]{1,0:T(8,128)S(1)} %shard_map.186.a), channel_id=1, source_target_pairs={{0,1},{1,0},{2,3},{3,2},{4,5},{5,4},{6,7},{7,6},{8,25},{9,24},{10,... | collective-permute-start | bytes 442376 | tf_op jit(solution)/shard_map/ppermute | solution.py:51
  43.6 9.0 %collective-permute-start.10 = (bf16[80,512]{1,0:T(8,128)(2,1)S(1)}, bf16[80,512]{1,0:T(8,128)(2,1)S(1)}, u32[]{:S(2)}, u32[]{:S(2)}) collective-permute-start(bf16[80,512]{1,0:T(8,128)(2,1)S(1)} %shard_map.187.a), channel_id=1, source_target_pairs={{0,17},{1,16},{2,19},{3,18},{4,21},{5,20},{6,23},{7,22},{8,57},{9,... | collective-permute-start | bytes 245768 | tf_op jit(solution)/shard_map/ppermute | solution.py:51
  52.6 4.5 %collective-permute-start.11 = (bf16[80,512]{1,0:T(8,128)(2,1)S(1)}, bf16[80,512]{1,0:T(8,128)(2,1)S(1)}, u32[]{:S(2)}, u32[]{:S(2)}) collective-permute-start(bf16[80,512]{1,0:T(8,128)(2,1)S(1)} %shard_map.188.a), channel_id=1, source_target_pairs={{0,49},{1,48},{2,51},{3,50},{4,53},{5,52},{6,55},{7,54},{8,9},{9,8... | collective-permute-start | bytes 245768 | tf_op jit(solution)/shard_map/ppermute | solution.py:51
  57.1 4.1 %collective-permute-start.14 = (bf16[64,512]{1,0:T(8,128)(2,1)S(1)}, bf16[64,512]{1,0:T(8,128)(2,1)S(1)}, u32[]{:S(2)}, u32[]{:S(2)}) collective-permute-start(bf16[64,512]{1,0:T(8,128)(2,1)S(1)} %get-tuple-element.47.refs_0_), channel_id=1, source_target_pairs={{0,198},{1,199},{2,196},{3,197},{4,194},{5,195},{6,192},{7,193},{8... | collective-permute-start | bytes 196616 | tf_op jit(solution)/shard_map/ppermute | solution.py:51
  58.6 3.4 %collective-permute-start.13 = (bf16[64,512]{1,0:T(8,128)(2,1)S(1)}, bf16[64,512]{1,0:T(8,128)(2,1)S(1)}, u32[]{:S(2)}, u32[]{:S(2)}) collective-permute-start(bf16[64,512]{1,0:T(8,128)(2,1)S(1)} %get-tuple-element.47.refs_0_), channel_id=1, source_target_pairs={{0,192},{1,193},{2,194},{3,195},{4,196},{5,197},{6,198},{7,199},{8... | collective-permute-start | bytes 196616 | tf_op jit(solution)/shard_map/ppermute | solution.py:51
  59.8 3.1 %collective-permute-start.12 = (bf16[64,512]{1,0:T(8,128)(2,1)S(1)}, bf16[64,512]{1,0:T(8,128)(2,1)S(1)}, u32[]{:S(2)}, u32[]{:S(2)}) collective-permute-start(bf16[64,512]{1,0:T(8,128)(2,1)S(1)} %get-tuple-element.47.refs_0_), channel_id=1, source_target_pairs={{0,6},{1,7},{2,4},{3,5},{4,2},{5,3},{6,0},{7,1},{8,10},{9,11},{10,... | collective-permute-start | bytes 196616 | tf_op jit(solution)/shard_map/ppermute | solution.py:51
  62.9 7.5 %collective-permute-start.17 = (bf16[256,512]{1,0:T(8,128)(2,1)S(1)}, bf16[256,512]{1,0:T(8,128)(2,1)S(1)}, u32[]{:S(2)}, u32[]{:S(2)}) collective-permute-start(bf16[256,512]{1,0:T(8,128)(2,1)S(1)} %shard_map.190.refs_0_), channel_id=1, source_target_pairs={{0,66},{1,67},{2,64},{3,65},{4,70},{5,71},{6,68},{7,69},{8,206},{9... | collective-permute-start | bytes 786440 | tf_op jit(solution)/shard_map/ppermute | solution.py:51
  63.6 11.3 %collective-permute-start.16 = (bf16[256,512]{1,0:T(8,128)(2,1)S(1)}, bf16[256,512]{1,0:T(8,128)(2,1)S(1)}, u32[]{:S(2)}, u32[]{:S(2)}) collective-permute-start(bf16[256,512]{1,0:T(8,128)(2,1)S(1)} %shard_map.190.refs_0_), channel_id=1, source_target_pairs={{0,64},{1,65},{2,66},{3,67},{4,68},{5,69},{6,70},{7,71},{8,200},{9... | collective-permute-start | bytes 786440 | tf_op jit(solution)/shard_map/ppermute | solution.py:51
  68.2 7.2 %collective-permute-start.15 = (bf16[256,512]{1,0:T(8,128)(2,1)S(1)}, bf16[256,512]{1,0:T(8,128)(2,1)S(1)}, u32[]{:S(2)}, u32[]{:S(2)}) collective-permute-start(bf16[256,512]{1,0:T(8,128)(2,1)S(1)} %shard_map.190.refs_0_), channel_id=1, source_target_pairs={{0,2},{1,3},{2,0},{3,1},{4,6},{5,7},{6,4},{7,5},{8,14},{9,15},{10,... | collective-permute-start | bytes 786440 | tf_op jit(solution)/shard_map/ppermute | solution.py:51
  75.4 28.9 %collective-permute-start.20 = (bf16[1040,512]{1,0:T(8,128)(2,1)S(1)}, bf16[1040,512]{1,0:T(8,128)(2,1)S(1)}, u32[]{:S(2)}, u32[]{:S(2)}) collective-permute-start(bf16[1040,512]{1,0:T(8,128)(2,1)S(1)} %shard_map.191.own), channel_id=1, source_target_pairs={{0,8},{1,9},{2,10},{3,11},{4,12},{5,13},{6,14},{7,15},{8,0},{9,1},... | collective-permute-start | bytes 3194888 | tf_op jit(solution)/shard_map/ppermute | solution.py:51
  90.6 7.5 %collective-permute-start.18 = (bf16[2,96,512]{2,1,0:T(8,128)(2,1)S(1)}, bf16[2,96,512]{2,1,0:T(8,128)(2,1)S(1)}, u32[]{:S(2)}, u32[]{:S(2)}) collective-permute-start(bf16[2,96,512]{2,1,0:T(8,128)(2,1)S(1)} %get-tuple-element.49), channel_id=1, source_target_pairs={{0,7},{1,0},{2,1},{3,2},{4,3},{5,4},{6,5},{7,6},{8,15},{9,8},{10,9... | collective-permute-start | bytes 589832 | tf_op jit(solution)/shard_map/ppermute | solution.py:394
  93.9 9.4 %collective-permute-start.19 = (bf16[2,96,512]{2,1,0:T(8,128)(2,1)S(1)}, bf16[2,96,512]{2,1,0:T(8,128)(2,1)S(1)}, u32[]{:S(2)}, u32[]{:S(2)}) collective-permute-start(bf16[2,96,512]{2,1,0:T(8,128)(2,1)S(1)} %get-tuple-element.50), channel_id=1, source_target_pairs={{0,1},{1,2},{2,3},{3,4},{4,5},{5,6},{6,7},{7,0},{8,9},{9,10},{10,1... | collective-permute-start | bytes 589832 | tf_op jit(solution)/shard_map/ppermute | solution.py:394
